TPU v7x, 32 devices: a whole 2x2x4 slice. The times are simulated.
32 devices in a mesh: dp: 4 (over x, core), expert: 8 (over z, y).
Axes of the slice: x: 2, y: 2, z: 4, core: 2. Of those that a mesh axis runs over, the one named last changes fastest.
Arguments:
- tokens: bfloat16 [16384, 768], P(('dp', 'expert')), may hold values from -6 to 6
- cotangent: bfloat16 [16384, 768], P(('dp', 'expert')), may hold values from -6 to 6
- chosen: int32 [16384, 2], P(('dp', 'expert')), may hold values from 0 to 9, all different within a row; in each aligned block of 512 rows (0 to 511, 512 to 1023, ...) at most 128 rows name the same one
- gates: float32 [16384, 2], P(('dp', 'expert')), may hold values from 0.2 to 0.8
- lengths: int32 [32, 8], P(('dp', 'expert')), may hold values from 1 to 256, 512 in all within a row
- keep_mask: int32 [16384], P(('dp', 'expert')), may hold values 0 or 1
- gain1: float32 [768], replicated, may hold values from 0.5 to 1.5
- w_qkv: bfloat16 [768, 2304], replicated, may hold values from -0.21875 to 0.21875
- w_o: bfloat16 [768, 768], replicated, may hold values from -0.875 to 0.875
- gain2: float32 [768], replicated, may hold values from 0.5 to 1.5
- frozen_in: bfloat16 [2, 3072, 768], replicated, may hold values from -0.21875 to 0.21875
- frozen_out: bfloat16 [2, 3072, 768], replicated, may hold values from -0.109375 to 0.109375
- w_in: bfloat16 [8, 3072, 768], P('expert', 'dp'), may hold values from -0.21875 to 0.21875
- w_out: bfloat16 [8, 3072, 768], P('expert', 'dp'), may hold values from -0.109375 to 0.109375
Outputs:
- output: bfloat16 [16384, 768], P(('dp', 'expert'))
- d_tokens: bfloat16 [16384, 768], P(('dp', 'expert'))
- d_gain1: float32 [768], replicated
- d_w_qkv: float32 [768, 2304], replicated
- d_w_o: float32 [768, 768], replicated
- d_gain2: float32 [768], replicated
- d_w_in: float32 [8, 3072, 768], P('expert', 'dp')
- d_w_out: float32 [8, 3072, 768], P('expert', 'dp')
- counts: float32 [10], replicated
Inputs may be any that keep to these rules, and one draw needn't show every extreme that they name: `chosen`: each token names two different experts; among the 512 tokens of one device no expert is named more than 128 times, a bound that some block reaches. The 8 lengths of a device sum to 512; the longest is exactly 256.
All inputs are finite; a program needn't handle non-finite values. No bound on the sum of `keep_mask` on one device may be relied on, other than what follows from the above.
Results may differ from a plain program's by a relative error of at most 0.012.
Values may be sent and summed in bfloat16 or wider, within the bound.
A program may use at most 256 MiB of HBM per device.

v0:
```python
import functools
import jax
import jax.numpy as jnp
from jax import lax
from jax.experimental import pallas as pl
from jax.experimental.pallas import tpu as pltpu
from jax.sharding import PartitionSpec as P

MESH = pl.DeviceIdType.MESH


def butterfly(dp_size, ex_size):
    core = ("dp", 1)
    xs = [("dp", 2 << k) for k in range((dp_size // 2).bit_length() - 1)]
    depth = 4 if ex_size % 4 == 0 else 1
    wide = ex_size // depth
    ys = [("expert", 1 << k) for k in range(wide.bit_length() - 1)]
    zs = [("expert", wide << k) for k in range(depth.bit_length() - 1)]
    return core, xs, ys, zs


def partner_of(step):
    axis, mask = step
    place = {"dp": lax.axis_index("dp"), "expert": lax.axis_index("expert")}
    bit = lax.rem(place[axis] // mask, 2)
    place[axis] = place[axis] + mask - 2 * mask * bit
    return bit, (place["dp"], place["expert"])


def reduce_kernel(dp_size, ex_size, w_ref, s_ref, out_ref, sum_ref, acc, got, small, ssem, rsem, gsem, hsem, tsem, usem):
    core, xs, ys, zs = butterfly(dp_size, ex_size)
    orders = [[core] + xs + ys + zs, [core] + ys + zs + xs, [core] + zs + xs + ys]
    count = len(orders[0])
    parts = len(orders)
    rows = w_ref.shape[0] // parts
    barrier = pltpu.get_barrier_semaphore()
    for step in orders[0]:
        _, peer = partner_of(step)
        pl.semaphore_signal(barrier, inc=1, device_id=peer, device_id_type=MESH)
    pl.semaphore_wait(barrier, count)

    offs = [[p * rows] for p in range(parts)]
    land = [[p * rows] for p in range(parts)]

    def scatter_send(p, i):
        bit, peer = partner_of(orders[p][i])
        half = rows >> (i + 1)
        source = w_ref if i == 0 else acc
        give = pl.multiple_of(offs[p][i] + (1 - bit) * half, half)
        copy = pltpu.make_async_remote_copy(
            src_ref=source.at[pl.ds(give, half)],
            dst_ref=got.at[pl.ds(land[p][i], half)],
            send_sem=ssem.at[p, i], recv_sem=rsem.at[p, i],
            device_id=peer, device_id_type=MESH)
        copy.start()
        offs[p].append(offs[p][i] + bit * half)
        land[p].append(land[p][i] + half)
        return copy

    def small_send(i):
        _, peer = partner_of(orders[0][i])
        copy = pltpu.make_async_remote_copy(
            src_ref=s_ref if i == 0 else small.at[count + i], dst_ref=small.at[i],
            send_sem=tsem.at[i], recv_sem=usem.at[i], device_id=peer, device_id_type=MESH)
        copy.start()
        return copy

    live = [scatter_send(p, 0) for p in range(parts)]
    tiny = small_send(0)
    for i in range(count):
        half = rows >> (i + 1)
        for p in range(parts):
            live[p].wait()
            source = w_ref if i == 0 else acc
            target = acc if i + 1 < count else out_ref
            keep = offs[p][i + 1]
            tile = min(half, 128)

            def add(j, _, keep=keep, start=land[p][i], source=source, target=target, tile=tile):
                at = pl.ds(pl.multiple_of(keep + j * tile, tile), tile)
                other = got[pl.ds(pl.multiple_of(start + j * tile, tile), tile), :]
                target[at, :] = (source[at, :].astype(jnp.float32) + other.astype(jnp.float32)).astype(jnp.bfloat16)
                return 0

            lax.fori_loop(0, half // tile, add, 0)
            if i + 1 < count:
                live[p] = scatter_send(p, i + 1)
        tiny.wait()
        mine = s_ref[...] if i == 0 else small[count + i]
        total = mine + small[i]
        if i + 1 < count:
            small[count + i + 1] = total
            tiny = small_send(i + 1)
        else:
            sum_ref[...] = total

    def gather_send(p, i):
        _, peer = partner_of(orders[p][i])
        half = rows >> (i + 1)
        at = pl.ds(pl.multiple_of(offs[p][i + 1], half), half)
        copy = pltpu.make_async_remote_copy(
            src_ref=out_ref.at[at], dst_ref=out_ref.at[at],
            send_sem=gsem.at[p, i], recv_sem=hsem.at[p, i], device_id=peer, device_id_type=MESH)
        copy.start()
        return copy

    for i in reversed(range(count)):
        live = [gather_send(p, i) for p in range(parts)]
        for p in range(parts):
            live[p].wait()


def all_reduce(blocks, small, dp_size, ex_size):
    steps = (dp_size * ex_size).bit_length() - 1
    rows, width = blocks.shape
    vmem = pl.BlockSpec(memory_space=pltpu.VMEM)
    dma = pltpu.SemaphoreType.DMA
    return pl.pallas_call(
        functools.partial(reduce_kernel, dp_size, ex_size),
        out_shape=(jax.ShapeDtypeStruct(blocks.shape, jnp.bfloat16), jax.ShapeDtypeStruct(small.shape, jnp.float32)),
        in_specs=[vmem, vmem],
        out_specs=(vmem, vmem),
        scratch_shapes=[
            pltpu.VMEM((rows, width), jnp.bfloat16),
            pltpu.VMEM((rows, width), jnp.bfloat16),
            pltpu.VMEM((2 * steps,) + small.shape, jnp.float32),
            dma((3, steps)), dma((3, steps)), dma((3, steps)), dma((3, steps)), dma((steps,)), dma((steps,)),
        ],
        compiler_params=pltpu.CompilerParams(collective_id=3, has_side_effects=True, vmem_limit_bytes=48 << 20),
        name="reduce_gradients",
    )(blocks, small)


def dot_nn(a, b):
    return jnp.dot(a, b, preferred_element_type=jnp.float32)


def dot_nt(a, b):
    return lax.dot_general(a, b, (((1,), (1,)), ((), ())), preferred_element_type=jnp.float32)


def dot_tn(a, b):
    return lax.dot_general(a, b, (((0,), (0,)), ((), ())), preferred_element_type=jnp.float32)


GELU_A = 0.7978845608028654
GELU_B = GELU_A * 0.044715


def gelu_pair(h):
    square = h * h
    bend = jnp.tanh(h * (GELU_B * square + GELU_A))
    share = 0.5 * bend + 0.5
    slope = share + (0.5 * h) * (1.0 - bend * bend) * ((3.0 * GELU_B) * square + GELU_A)
    return h * share, slope


def expert_kernel(dp_size, ex_size, cap, rows_hbm, fgrad_hbm, agrad_hbm, win_hbm, shard_hbm, fin_hbm, fout_hbm,
                  back_hbm, res_hbm, dw_hbm,
                  rows_v, grad_v, win_v, wout_v, act_v, hg_v, fin_v, fout_v, frow_v, fgrad_v, facc_v, fout_st,
                  rg_v, dw_st, send_row, recv_row, send_back, recv_back, send_w, recv_w, fwd_w, got_w,
                  load_sem, frozen_sem, fload_sem, store_sem, dw_sem):
    dp = lax.axis_index("dp")
    ex = lax.axis_index("expert")
    shard = shard_hbm.shape[0]
    feat = shard_hbm.shape[1]
    slots = ex_size * cap
    far = dp_size // 2
    tiles = win_hbm.shape[0] // 256
    span = fin_v.shape[1]
    steps = fin_hbm.shape[0]

    barrier = pltpu.get_barrier_semaphore()
    for r in range(1, ex_size):
        pl.semaphore_signal(barrier, inc=1, device_id=(dp, ex ^ r), device_id_type=MESH)
    pl.semaphore_signal(barrier, inc=1, device_id=(dp ^ 1, ex), device_id_type=MESH)
    for k in range(1, far):
        pl.semaphore_signal(barrier, inc=1, device_id=(dp ^ (2 * k), ex), device_id_type=MESH)
    local = [
        pltpu.make_async_copy(rows_hbm.at[pl.ds(0, 2)], frow_v, load_sem.at[0]),
        pltpu.make_async_copy(fgrad_hbm, fgrad_v, load_sem.at[1]),
    ]
    for copy in local:
        copy.start()

    def frozen_load(i, slot):
        return (pltpu.make_async_copy(fin_hbm.at[i], fin_v.at[slot], frozen_sem.at[0, slot]),
                pltpu.make_async_copy(fout_hbm.at[i], fout_v.at[slot], frozen_sem.at[1, slot]))

    for copy in frozen_load(0, 0):
        copy.start()
    pl.semaphore_wait(barrier, ex_size - 1 + 1 + far - 1)

    row_copies = []
    for r in reversed(range(1, ex_size)):
        copy = pltpu.make_async_remote_copy(
            src_ref=rows_hbm.at[2 + (ex ^ r)], dst_ref=rows_v.at[pl.ds(r * cap, cap)],
            send_sem=send_row.at[r], recv_sem=recv_row.at[r], device_id=(dp, ex ^ r), device_id_type=MESH)
        copy.start()
        row_copies.append(copy)
    own = [pltpu.make_async_copy(rows_hbm.at[2 + ex], rows_v.at[pl.ds(0, cap)], load_sem.at[2]),
           pltpu.make_async_copy(win_hbm, win_v, load_sem.at[3]),
           pltpu.make_async_copy(shard_hbm, wout_v.at[pl.ds(pl.multiple_of(dp * shard, shard), shard)], load_sem.at[4])]
    for copy in own:
        copy.start()

    mine = wout_v.at[pl.ds(pl.multiple_of(dp * shard, shard), shard)]
    weight_copies = []
    for k in range(1, far):
        copy = pltpu.make_async_remote_copy(
            src_ref=shard_hbm, dst_ref=mine, send_sem=send_w.at[k], recv_sem=recv_w.at[k],
            device_id=(dp ^ (2 * k), ex), device_id_type=MESH)
        copy.start()
        weight_copies.append(copy)
    beside = pltpu.make_async_remote_copy(
        src_ref=shard_hbm, dst_ref=mine, send_sem=send_w.at[0], recv_sem=recv_w.at[0],
        device_id=(dp ^ 1, ex), device_id_type=MESH)
    beside.start()
    grad_copies = []
    for r in range(ex_size):
        copy = pltpu.make_async_copy(agrad_hbm.at[ex ^ r], grad_v.at[pl.ds(r * cap, cap)], fload_sem.at[r])
        copy.start()
        grad_copies.append(copy)

    for copy in local:
        copy.wait()
    per = steps // 2

    def frozen(i, _):
        slot = lax.rem(i, 2)
        for copy in frozen_load(i, slot):
            copy.wait()

        @pl.when(i + 1 < steps)
        def _():
            for copy in frozen_load(i + 1, 1 - slot):
                copy.start()
        which = i // per
        up = fin_v[slot]
        down = fout_v[slot]
        hidden = dot_nt(frow_v[which], up)
        slope_in = dot_nt(fgrad_v[which], down)
        active, slope = gelu_pair(hidden)
        result = dot_nn(active.astype(jnp.bfloat16), down)
        back = dot_nn((slope_in * slope).astype(jnp.bfloat16), up)
        first = lax.rem(i, per) == 0

        @pl.when(first)
        def _():
            facc_v[0, which] = result
            facc_v[1, which] = back

        @pl.when(jnp.logical_not(first))
        def _():
            facc_v[0, which] += result
            facc_v[1, which] += back
        return 0

    lax.fori_loop(0, steps, frozen, 0)
    fout_st[...] = facc_v[...].astype(jnp.bfloat16)
    stores = [pltpu.make_async_copy(fout_st.at[0], res_hbm.at[pl.ds(0, 2)], store_sem.at[0]),
              pltpu.make_async_copy(fout_st.at[1], back_hbm.at[pl.ds(0, 2)], store_sem.at[1])]
    for copy in stores:
        copy.start()

    passed = []
    for k in range(1, far):
        weight_copies[k - 1].wait_recv()
        theirs = wout_v.at[pl.ds(pl.multiple_of((dp ^ (2 * k)) * shard, shard), shard)]
        copy = pltpu.make_async_remote_copy(
            src_ref=theirs, dst_ref=theirs, send_sem=fwd_w.at[k], recv_sem=got_w.at[k],
            device_id=(dp ^ 1, ex), device_id_type=MESH)
        copy.start()
        passed.append(copy)
    beside.wait_recv()
    for copy in passed:
        copy.wait_recv()
    for copy in grad_copies:
        copy.wait()
    for copy in own:
        copy.wait()

    def slope_tile(t, _):
        at = pl.ds(pl.multiple_of(t * 256, 256), 256)
        hg_v[:, at] = dot_nt(grad_v[...], wout_v[at, :]).astype(jnp.bfloat16)
        return 0

    lax.fori_loop(0, tiles, slope_tile, 0)
    back_copies = []
    half = slots // 2
    for part in (1, 0):
        here = pl.ds(part * half, half)
        group = range(part * (ex_size // 2), (part + 1) * (ex_size // 2))
        for r in group:
            if r:
                row_copies[ex_size - 1 - r].wait_recv()

        def hidden_tile(t, _, here=here):
            at = pl.ds(pl.multiple_of(t * 256, 256), 256)
            active, slope = gelu_pair(dot_nt(rows_v[here, :], win_v[at, :]))
            act_v[here, at] = active.astype(jnp.bfloat16)
            hg_v[here, at] = (hg_v[here, at].astype(jnp.float32) * slope).astype(jnp.bfloat16)
            return 0

        lax.fori_loop(0, tiles, hidden_tile, 0)

        def back_tile(n, _, here=here):
            at = pl.ds(pl.multiple_of(n * 256, 256), 256)
            rg_v[here, at] = dot_nn(hg_v[here, :], win_v[:, at]).astype(jnp.bfloat16)
            return 0

        lax.fori_loop(0, feat // 256, back_tile, 0)
        for r in reversed(group):
            source = rg_v.at[pl.ds(r * cap, cap)]
            if r:
                copy = pltpu.make_async_remote_copy(
                    src_ref=source, dst_ref=back_hbm.at[2 + ex], send_sem=send_back.at[r], recv_sem=recv_back.at[r],
                    device_id=(dp, ex ^ r), device_id_type=MESH)
            else:
                copy = pltpu.make_async_copy(source, back_hbm.at[2 + ex], store_sem.at[2])
            copy.start()
            back_copies.append(copy)

    def result_tile(n, _):
        at = pl.ds(pl.multiple_of(n * 256, 256), 256)
        grad_st[:, at] = dot_nn(act_v[...], wout_v[:, at]).astype(jnp.bfloat16)
        return 0

    def weight_tile(t, _):
        at = pl.ds(pl.multiple_of(t * 256, 256), 256)
        slot = lax.rem(t, 2)

        @pl.when(t >= 2)
        def _():
            pltpu.make_async_copy(dw_st.at[slot], dw_hbm.at[at], dw_sem.at[slot]).wait()
        dw_st[slot, :, 0:feat] = dot_tn(hg_v[:, at], rows_v[...]).astype(jnp.bfloat16)
        dw_st[slot, :, feat:] = dot_tn(act_v[:, at], grad_v[...]).astype(jnp.bfloat16)
        pltpu.make_async_copy(dw_st.at[slot], dw_hbm.at[at], dw_sem.at[slot]).start()
        return 0

    lax.fori_loop(0, tiles, weight_tile, 0)
    grad_st = grad_v
    lax.fori_loop(0, feat // 256, result_tile, 0)
    res_copies = []
    for r in range(ex_size):
        copy = pltpu.make_async_copy(grad_st.at[pl.ds(r * cap, cap)], res_hbm.at[2 + (ex ^ r)], fload_sem.at[r])
        copy.start()
        res_copies.append(copy)
    for slot in range(2):
        pltpu.make_async_copy(dw_st.at[slot], dw_hbm.at[pl.ds(0, 256)], dw_sem.at[slot]).wait()
    for copy in res_copies + stores:
        copy.wait()
    for copy in weight_copies:
        copy.wait_send()
    beside.wait_send()
    for copy in passed:
        copy.wait_send()
    for copy in row_copies:
        copy.wait_send()
    for copy in back_copies:
        copy.wait()


def experts(rows, fgrad, agrad, win, shard, fin, fout, dp_size, ex_size):
    kinds, cap, feat = rows.shape
    hidden = win.shape[0]
    slots = ex_size * cap
    far = dp_size // 2
    span = 768 if hidden % 768 == 0 else hidden
    steps = 2 * hidden // span
    anyspace = pl.BlockSpec(memory_space=pl.ANY)
    dma = pltpu.SemaphoreType.DMA
    low = jnp.bfloat16
    return pl.pallas_call(
        functools.partial(expert_kernel, dp_size, ex_size, cap),
        out_shape=(jax.ShapeDtypeStruct((kinds, cap, feat), low), jax.ShapeDtypeStruct((kinds, cap, feat), low),
                   jax.ShapeDtypeStruct((hidden, 2 * feat), low)),
        in_specs=[anyspace] * 7,
        out_specs=(anyspace,) * 3,
        scratch_shapes=[
            pltpu.VMEM((slots, feat), low), pltpu.VMEM((slots, feat), low),
            pltpu.VMEM((hidden, feat), low), pltpu.VMEM((hidden, feat), low),
            pltpu.VMEM((slots, hidden), low), pltpu.VMEM((slots, hidden), low),
            pltpu.VMEM((2, span, feat), low), pltpu.VMEM((2, span, feat), low),
            pltpu.VMEM((2, cap, feat), low), pltpu.VMEM((2, cap, feat), low),
            pltpu.VMEM((2, 2, cap, feat), jnp.float32), pltpu.VMEM((2, 2, cap, feat), low),
            pltpu.VMEM((slots, feat), low), pltpu.VMEM((2, 256, 2 * feat), low),
            dma((ex_size,)), dma((ex_size,)), dma((ex_size,)), dma((ex_size,)),
            dma((far,)), dma((far,)), dma((far,)), dma((far,)),
            dma((5,)), dma((2, 2)), dma((ex_size,)), dma((3,)), dma((2,)),
        ],
        compiler_params=pltpu.CompilerParams(collective_id=1, has_side_effects=True, vmem_limit_bytes=60 << 20),
        name="experts",
    )(rows, fgrad, agrad, win, shard, fin.reshape(steps, span, feat), fout.reshape(steps, span, feat))


HEADS = 12
HEAD_DIM = 64
FROZEN = 2


def layer_norm(values_in, gain_vec):
    row_mean = jnp.mean(values_in, axis=-1, keepdims=True)
    centred = values_in - row_mean
    variance = jnp.mean(centred * centred, axis=-1, keepdims=True)
    return centred * lax.rsqrt(variance + 1e-05) * gain_vec


def block_scores(query_part, key_heads, allowed):
    scores = (
        jnp.einsum("qhd,khd->hqk", query_part, key_heads, preferred_element_type=jnp.float32)
        * 0.125
    )
    return jnp.where(allowed[None], scores, -1e30)


def body(
    tokens,
    cotangent,
    chosen,
    gates,
    lengths,
    keep_mask,
    gain1,
    w_qkv,
    w_o,
    gain2,
    frozen_in,
    frozen_out,
    w_in,
    w_out,
):
    row_count = tokens.shape[0]
    feat_width = tokens.shape[1]
    owners = lax.axis_size("expert")
    kind_count = FROZEN + owners
    slot_count = ((2 * row_count * 5 // (4 * kind_count) + 7) // 8 * 8 + 15) // 16 * 16
    block_rows = min(512, row_count)
    weights_in = lax.all_gather(w_in, "dp", axis=1, tiled=True)[0]
    tokens_full = tokens.astype(jnp.float32)
    normed_one, norm_one_back = jax.vjp(layer_norm, tokens_full, gain1)
    normed_one_low = normed_one.astype(jnp.bfloat16)
    projected = jnp.dot(normed_one_low, w_qkv, preferred_element_type=jnp.float32).astype(
        jnp.bfloat16
    )
    queries = projected[:, :feat_width].reshape(row_count, HEADS, HEAD_DIM)
    key_heads = projected[:, feat_width : 2 * feat_width].reshape(row_count, HEADS, HEAD_DIM)
    value_heads = projected[:, 2 * feat_width :].reshape(row_count, HEADS, HEAD_DIM)
    places = jnp.arange(row_count, dtype=jnp.int32)
    doc_ends = jnp.cumsum(lengths[0])
    documents = jnp.sum((places[:, None] >= doc_ends[None, :]).astype(jnp.int32), axis=1)

    def permitted():
        return (
            (documents[:, None] == documents[None, :])
            & (places[None, :] <= places[:, None])
            & ((keep_mask[None, :] > 0) | (places[None, :] == places[:, None]))
        )

    scores = block_scores(queries, key_heads, permitted())
    peak_score = jnp.max(scores, axis=-1, keepdims=True)
    exp_scores = jnp.exp(scores - peak_score)
    exp_total = jnp.sum(exp_scores, axis=-1, keepdims=True)
    probs_low = (exp_scores / exp_total).astype(jnp.bfloat16)
    block_out = jnp.einsum(
        "hqk,khd->qhd", probs_low, value_heads, preferred_element_type=jnp.float32
    )
    out_blocks = block_out.reshape(block_rows, feat_width).astype(jnp.bfloat16)
    lse_blocks = [peak_score + jnp.log(exp_total)]
    mixed_rows = tokens_full + jnp.dot(out_blocks, w_o, preferred_element_type=jnp.float32)
    normed_two, norm_two_back = jax.vjp(layer_norm, mixed_rows, gain2)
    normed_two_low = normed_two.astype(jnp.bfloat16)
    flat_ids = chosen.reshape(-1)
    one_hot = (flat_ids[:, None] == jnp.arange(kind_count, dtype=jnp.int32)[None, :]).astype(
        jnp.int32
    )
    slot_ranks = jnp.sum(jnp.cumsum(one_hot, axis=0) * one_hot, axis=1) - 1
    positions = flat_ids * slot_count + slot_ranks
    buffer_rows = (
        jnp.zeros((kind_count * slot_count, feat_width), jnp.bfloat16)
        .at[positions]
        .set(jnp.repeat(normed_two_low, 2, axis=0))
    )
    grad_out = cotangent.astype(jnp.float32)
    weighted = (jnp.repeat(grad_out, 2, axis=0) * gates.reshape(-1, 1)).astype(jnp.bfloat16)
    grad_buffer = (
        jnp.zeros((kind_count * slot_count, feat_width), jnp.bfloat16).at[positions].set(weighted)
    )
    dp_size = lax.axis_size("dp")
    grad_slots = grad_buffer.reshape(kind_count, slot_count, feat_width)
    arrived_grad = lax.all_to_all(grad_slots[FROZEN:], "expert", split_axis=0, concat_axis=0, tiled=True)
    row_grads, served, weight_grads = experts(
        buffer_rows.reshape(kind_count, slot_count, feat_width), grad_slots[:FROZEN], arrived_grad,
        weights_in, w_out[0], frozen_in, frozen_out, dp_size, owners)
    returned = lax.all_to_all(served[FROZEN:], "expert", split_axis=0, concat_axis=0, tiled=True)
    results = jnp.concatenate([served[:FROZEN], returned], axis=0).reshape(-1, feat_width)
    picked = results[positions].astype(jnp.float32).reshape(row_count, 2, feat_width)
    output = mixed_rows + jnp.sum(picked * gates[:, :, None], axis=1)
    summed = lax.psum_scatter(
        weight_grads, "dp", scatter_dimension=0, tiled=True
    ).astype(jnp.float32)
    d_w_in = summed[:, :feat_width][None]
    d_w_out = summed[:, feat_width:][None]
    row_grads = row_grads.reshape(-1, feat_width)
    normed_two_grad = jnp.sum(
        row_grads[positions].astype(jnp.float32).reshape(row_count, 2, feat_width), axis=1
    )
    mixed_part, gain2_grad = norm_two_back(normed_two_grad)
    mixed_grad = grad_out + mixed_part
    branch_grad = mixed_grad.astype(jnp.bfloat16)
    w_o_grad = lax.dot_general(
        out_blocks, branch_grad, (((0,), (0,)), ((), ())), preferred_element_type=jnp.float32
    )
    attended_grad = lax.dot_general(
        branch_grad, w_o, (((1,), (1,)), ((), ())), preferred_element_type=jnp.float32
    ).astype(jnp.bfloat16)
    attended_heads = attended_grad.reshape(row_count, HEADS, HEAD_DIM)
    key_grad = jnp.zeros((row_count, HEADS, HEAD_DIM), jnp.float32)
    value_grad = jnp.zeros((row_count, HEADS, HEAD_DIM), jnp.float32)
    query_grads = []
    for block_index, row_start in enumerate(range(0, row_count, block_rows)):
        scores = block_scores(queries, key_heads, permitted())
        probs_full = jnp.exp(scores - lse_blocks[block_index])
        probs_low = probs_full.astype(jnp.bfloat16)
        prob_grad = jnp.einsum(
            "qhd,khd->hqk", attended_heads, value_heads, preferred_element_type=jnp.float32
        )
        row_delta = jnp.sum(probs_full * prob_grad, axis=-1, keepdims=True)
        score_grad = (probs_full * (prob_grad - row_delta)).astype(jnp.bfloat16)
        query_grads.append(
            jnp.einsum("hqk,khd->qhd", score_grad, key_heads, preferred_element_type=jnp.float32)
            * 0.125
        )
        key_grad = (
            jnp.einsum("hqk,qhd->khd", score_grad, queries, preferred_element_type=jnp.float32)
            * 0.125
        )
        value_grad = jnp.einsum(
            "hqk,qhd->khd", probs_low, attended_heads, preferred_element_type=jnp.float32
        )
    projected_grad = jnp.concatenate(
        [
            query_grads[0].reshape(row_count, feat_width),
            key_grad.reshape(row_count, feat_width),
            value_grad.reshape(row_count, feat_width),
        ],
        axis=1,
    ).astype(jnp.bfloat16)
    w_qkv_grad = lax.dot_general(
        normed_one_low, projected_grad, (((0,), (0,)), ((), ())), preferred_element_type=jnp.float32
    )
    normed_one_grad = lax.dot_general(
        projected_grad, w_qkv, (((1,), (1,)), ((), ())), preferred_element_type=jnp.float32
    )
    tokens_part, gain1_grad = norm_one_back(normed_one_grad)
    tokens_grad = (mixed_grad + tokens_part).astype(jnp.bfloat16)
    local_counts = jnp.sum(one_hot, axis=0).astype(jnp.float32)
    both = jnp.concatenate([w_qkv_grad, w_o_grad], axis=1).astype(jnp.bfloat16)
    half = feat_width // 2
    blocks = both.reshape(feat_width, 8, half).transpose(1, 0, 2).reshape(8 * feat_width, half)
    padded_counts = jnp.pad(local_counts, (0, feat_width - kind_count))
    small = jnp.concatenate(
        [gain1_grad[None], gain2_grad[None], padded_counts[None], jnp.zeros((5, feat_width), jnp.float32)])
    total, small_sum = all_reduce(blocks, small, lax.axis_size("dp"), owners)
    both_sum = total.reshape(8, feat_width, half).transpose(1, 0, 2).reshape(feat_width, 8 * half)
    w_qkv_sum = both_sum[:, : 3 * feat_width].astype(jnp.float32)
    w_o_sum = both_sum[:, 3 * feat_width :].astype(jnp.float32)
    gain1_sum, gain2_sum, counts = small_sum[0], small_sum[1], small_sum[2, :kind_count]
    return (
        output.astype(jnp.bfloat16),
        tokens_grad,
        gain1_sum,
        w_qkv_sum,
        w_o_sum,
        gain2_sum,
        d_w_in,
        d_w_out,
        counts,
    )


def solution(mesh):
    placed = (
        P(("dp", "expert"), None),
        P(("dp", "expert"), None),
        P(("dp", "expert"), None),
        P(("dp", "expert"), None),
        P(("dp", "expert"), None),
        P(("dp", "expert")),
        P(),
        P(),
        P(),
        P(),
        P(),
        P(),
        P("expert", "dp", None),
        P("expert", "dp", None),
    )
    return jax.shard_map(
        body,
        mesh=mesh,
        in_specs=placed,
        out_specs=(
            P(("dp", "expert"), None),
            P(("dp", "expert"), None),
            P(),
            P(),
            P(),
            P(),
            P("expert", "dp", None),
            P("expert", "dp", None),
            P(),
        ),
        check_vma=False,
    )
```

profile of v0, /device:TPU:0, one launch (start us, length us, event | category | flops | bytes accessed | tf_op | source)
XLA Modules:
  0.0 408.0 jit_solution(1022398535963525723)
XLA Ops:
  17.7 6.2 %reduce-window.19 = s32[10,8,128]{2,1,0:T(8,128)} reduce-window(s32[10,8,128]{2,1,0:T(8,128)} %fusion.33, s32[]{:T(128)} %constant.36.clone.1), window={size=1x1x128 pad=0_0x0_0x127_0}, to_apply=%region_6.7 | reduce-window | flops 1300480 | bytes 81924 | tf_op jit(solution)/shard_map/reduce-window.1
  31.2 3.6 broadcast_in_dim.39
  34.8 5.3 %reshape.315 = f32[1024,768]{1,0:T(8,128)} reshape(f32[512,2,768]{2,1,0:T(2,128)} %broadcast_in_dim.39) | data formatting | bytes 6291456 | tf_op jit(solution)/shard_map/reshape | solution.py:485
  40.1 7.9 %scatter_custom_fusion.1 = bf16[1280,768]{1,0:T(8,128)(2,1)} fusion(s32[1024]{0:T(1024)S(1)} %bitcast.103, f32[1024,768]{1,0:T(8,128)} %reshape.315, f32[1024]{0:T(1024)S(1)} %mul.180, bf16[]{:T(256)} %constant.40.clone.1), kind=kCustom, calls=%fused_computation.42 | custom fusion | flops 1572864 | bytes 5115906 | tf_op jit(solution)/shard_map/scatter | solution.py:487
  48.0 2.7 slice.82
  50.6 7.5 %all-to-all-start = ((bf16[8,128,768]{2,1,0:T(8,128)(2,1)}), bf16[8,128,768]{2,1,0:T(8,128)(2,1)}, u32[]{:S(2)}, u32[]{:S(2)}) async-start(bf16[8,128,768]{2,1,0:T(8,128)(2,1)} %bitcast.89), calls=%async_computation | async-start | bytes 3145728 | tf_op jit(solution)/shard_map/all_to_all | solution.py:491
  63.8 3.3 convolution_convert_fusion.1
  68.5 2.3 copy.61
  75.8 3.5 fusion.6
  79.4 3.7 fusion
  84.1 5.1 %fusion.22 = bf16[12,64,512]{2,1,0:T(8,128)(2,1)S(1)} fusion(bf16[512,12,64]{0,2,1:T(8,128)(2,1)} %bitcast.91, f32[12,512]{1,0:T(8,128)S(1)} %fusion, f32[12,512]{1,0:T(8,128)S(1)} %get-tuple-element.35, f32[12,512,512]{1,2,0:T(8,128)S(1)} %get-tuple-element.36, pred[512,512]{0,1:T(8,128)(4,1)} %copy-done.9), kind=kOutput, calls=%fused_computation.56 | convolution fusion | flops 418775040 | bytes 14467072 | tf_op jit(solution)/shard_map/hqk,khd->qhd/dot_general | solution.py:465
  93.7 4.6 %reshape.351 = bf16[1024,768]{1,0:T(8,128)(2,1)} reshape(bf16[512,2,768]{2,1,0:T(2,128)(2,1)} %broadcast_in_dim.38) | data formatting | bytes 3145728 | tf_op jit(solution)/shard_map/reshape | solution.py:482
  98.3 7.2 %scatter_custom_fusion = bf16[1280,768]{1,0:T(8,128)(2,1)} fusion(s32[1024]{0:T(1024)} %bitcast.104, bf16[1024,768]{1,0:T(8,128)(2,1)} %reshape.351, bf16[]{:T(256)} %constant.40.clone.1), kind=kCustom, calls=%fused_computation.64 | custom fusion | bytes 1966592 | tf_op jit(solution)/shard_map/scatter | solution.py:482
  105.5 84.9 %experts.1 = (bf16[10,128,768]{2,1,0:T(8,128)(2,1)}, bf16[10,128,768]{2,1,0:T(8,128)(2,1)}, bf16[3072,1536]{1,0:T(8,128)(2,1)}) custom-call(bf16[10,128,768]{2,1,0:T(8,128)(2,1)} %bitcast.86, bf16[2,128,768]{2,1,0:T(8,128)(2,1)} %bitcast.97, bf16[8,128,768]{2,1,0:T(8,128)(2,1)} %all-to-all-done.agrad_hbm, bf16[3072,768]{1,0:T(8,128)(2,1)} %bitcast.90, ...), custom_call_target="tpu_custom_call" | custom-call | tf_op jit(solution)/shard_map/experts/pallas_call | solution.py:374
  190.5 2.7 slice.64
  193.1 4.6 %all-to-all-start.1 = ((bf16[8,128,768]{2,1,0:T(8,128)(2,1)}), bf16[8,128,768]{2,1,0:T(8,128)(2,1)}, u32[]{:S(2)}, u32[]{:S(2)}) async-start(bf16[8,128,768]{2,1,0:T(8,128)(2,1)} %slice.64), calls=%async_computation.1 | async-start | bytes 3145728 | tf_op jit(solution)/shard_map/all_to_all | solution.py:495
  202.9 7.9 %gather_fusion.1 = bf16[1024,768]{1,0:T(8,128)(2,1)} fusion(bf16[1280,768]{1,0:T(8,128)(2,1)} %bitcast.77, s32[1024]{0:T(1024)S(1)} %broadcast_clamp_fusion), kind=kCustom, calls=%fused_computation.1 | custom fusion | bytes 3149824 | tf_op jit(solution)/shard_map/gather | solution.py:506
  210.8 4.9 %reshape.330 = f32[512,2,768]{2,1,0:T(2,128)} reshape(bf16[1024,768]{1,0:T(8,128)(2,1)} %gather_fusion.1) | data formatting | bytes 4718592 | tf_op jit(solution)/shard_map/convert_element_type | solution.py:506
  215.6 6.8 %reduce_sum.185 = f32[512,768]{1,0:T(8,128)} reduce(f32[512,2,768]{2,1,0:T(2,128)} %reshape.330, f32[]{:T(128)} %constant.15.clone.1), dimensions={1}, to_apply=%region_14.15 | reduce | flops 393216 | bytes 4718596 | tf_op jit(solution)/shard_map/reduce_sum | solution.py:505
  222.4 2.5 multiply_reduce_fusion.2
  226.1 10.2 %all-to-all-done.1 = bf16[8,128,768]{2,1,0:T(8,128)(2,1)} async-done(((bf16[8,128,768]{2,1,0:T(8,128)(2,1)}), bf16[8,128,768]{2,1,0:T(8,128)(2,1)}, u32[]{:S(2)}, u32[]{:S(2)}) %all-to-all-start.1) | async-done | bytes 1572896 | tf_op jit(solution)/shard_map/all_to_all | solution.py:495
  236.3 3.1 pad_maximum_fusion.2
  239.3 7.4 %gather_fusion = bf16[1024,768]{1,0:T(8,128)(2,1)} fusion(bf16[1280,768]{1,0:T(8,128)(2,1)} %bitcast.76, s32[1024]{0:T(1024)S(1)} %broadcast_clamp_fusion), kind=kCustom, calls=%fused_computation | custom fusion | bytes 3149824 | tf_op jit(solution)/shard_map/gather | solution.py:497
  246.7 4.9 %reshape.329 = f32[512,2,768]{2,1,0:T(2,128)} reshape(bf16[1024,768]{1,0:T(8,128)(2,1)} %gather_fusion) | data formatting | bytes 4718592 | tf_op jit(solution)/shard_map/convert_element_type | solution.py:497
  251.6 16.6 %multiply_reduce_fusion.1 = f32[512,768]{1,0:T(8,128)S(1)} fusion(f32[512,2,768]{2,1,0:T(2,128)} %reshape.329, f32[512,2]{1,0:T(8,128)} %copy.68), kind=kLoop, calls=%fused_computation.21 | loop fusion | flops 1179648 | bytes 4722688 | tf_op jit(solution)/shard_map/reduce_sum | solution.py:498
  275.0 13.5 %multiply_reduce_fusion = (f32[12,512]{1,0:T(8,128)S(1)}, f32[12,512,512]{1,2,0:T(8,128)}) fusion(f32[12,512]{1,0:T(8,128)} %log_add_fusion, f32[12,512,512]{1,2,0:T(8,128)} %copy-done.1, pred[512,512]{0,1:T(8,128)(4,1)} %copy-done.9, bf16[512,12,64]{0,2,1:T(8,128)(2,1)} %bitcast.93, bf16[512,12,64]{0,2,1:T(8,128)(2,1)} %bitcast.92), kind=kOutput, calls=%fused_computation.5 | convolution fusion | flops 418375680 | bytes 27049984 | tf_op jit(solution)/shard_map/qhd,khd->hqk/dot_general | solution.py:525
  288.6 7.3 %multiply_convert_fusion = bf16[12,512,512]{1,2,0:T(8,128)(2,1)S(1)} fusion(f32[12,512,512]{1,2,0:T(8,128)} %get-tuple-element.40, f32[12,512]{1,0:T(8,128)S(1)} %get-tuple-element.39, f32[12,512]{1,0:T(8,128)S(1)} %copy-done.17, f32[12,512,512]{1,2,0:T(8,128)S(1)} %bitcast.75, pred[512,512]{0,1:T(8,128)(4,1)S(1)} %copy-done.10), kind=kLoop, calls=%fused_computation.4 | loop fusion | flops 18874368 | bytes 31768576 | tf_op jit(solution)/shard_map/convert_element_type | solution.py:529
  299.1 3.2 fusion.19
  311.2 2.7 copy.86
  314.0 73.0 %reduce_gradients.1 = (bf16[6144,384]{1,0:T(8,128)(2,1)S(1)}, f32[8,768]{1,0:T(8,128)S(1)}) custom-call(bf16[6144,384]{1,0:T(8,128)(2,1)} %bitcast.78, f32[8,768]{1,0:T(8,128)S(1)} %maximum_maximum_fusion.s_ref), custom_call_target="tpu_custom_call" | custom-call | tf_op jit(solution)/shard_map/reduce_gradients/pallas_call | solution.py:118
  392.3 3.5 slice_convert_fusion
  398.1 2.6 slice_bitcast_fusion
  (173 shorter events, 67.8 us)
Async XLA Ops:
  7.2 56.6 %copy-start = (bf16[768,2304]{1,0:T(8,128)(2,1)S(1)}, bf16[768,2304]{1,0:T(8,128)(2,1)}, u32[]{:S(2)}) copy-start(bf16[768,2304]{1,0:T(8,128)(2,1)} %param.21) | copy-start | bytes 10616836
  7.2 7.9 %copy-start.34 = (f32[512,2]{0,1:T(2,128)S(1)}, f32[512,2]{0,1:T(2,128)}, u32[]{:S(2)}) copy-start(f32[512,2]{0,1:T(2,128)} %param.17) | copy-start | bytes 12292
  7.2 98.3 %all-gather.2.cloned.1.call-start = ((), (), s32[]{:S(2)}) async-start(), calls=%async_computation.3 | async-start | bytes 5898240 | tf_op jit(solution)/shard_map/all_gather | solution.py:439
  40.1 7.9 %copy-start.28 = (s32[1024,1]{0,1:T(1,128)}, s32[1024,1]{0,1:T(1,128)S(1)}, u32[]{:S(2)}) copy-start(s32[1024,1]{0,1:T(1,128)S(1)} %compare_select_fusion) | copy-start | bytes 12292
  50.6 9.6 %copy-start.40 = (s32[1,8]{1,0:T(1,128)S(1)}, s32[1,8]{1,0:T(1,128)}, u32[]{:S(2)}) copy-start(s32[1,8]{1,0:T(1,128)} %param.18) | copy-start | bytes 100
  50.6 54.9 %all-to-all-start = ((bf16[8,128,768]{2,1,0:T(8,128)(2,1)}), bf16[8,128,768]{2,1,0:T(8,128)(2,1)}, u32[]{:S(2)}, u32[]{:S(2)}) async-start(bf16[8,128,768]{2,1,0:T(8,128)(2,1)} %bitcast.89), calls=%async_computation | async-start | bytes 3145728 | tf_op jit(solution)/shard_map/all_to_all | solution.py:491
  58.2 5.6 %copy-start.29 = (f32[768]{0:T(1024)S(1)}, f32[768]{0:T(1024)}, u32[]{:S(2)}) copy-start(f32[768]{0:T(1024)} %param.20) | copy-start | bytes 9220
  58.2 337.6 %reduce-scatter.2.cloned.1.call-start = ((), (), s32[]{:S(2)}) async-start(), calls=%async_computation.4 | async-start | bytes 11796480 | tf_op jit(solution)/shard_map/reduce_scatter | solution.py:499
  63.8 3.3 copy-start.22
  70.8 4.7 %copy-start.35 = (s32[512]{0:T(512)S(1)}, s32[512]{0:T(512)}, u32[]{:S(2)}) copy-start(s32[512]{0:T(512)} %param.19) | copy-start | bytes 6148
  75.8 3.5 copy-start.9
  79.4 4.6 %copy-start.1 = (f32[12,512,512]{1,2,0:T(8,128)}, f32[12,512,512]{1,2,0:T(8,128)S(1)}, u32[]{:S(2)}) copy-start(f32[12,512,512]{1,2,0:T(8,128)S(1)} %get-tuple-element.36) | copy-start | bytes 37748740
  79.4 4.7 %copy-start.16 = (f32[12,512]{1,0:T(8,128)}, f32[12,512]{1,0:T(8,128)S(1)}, u32[]{:S(2)}) copy-start(f32[12,512]{1,0:T(8,128)S(1)} %get-tuple-element.35) | copy-start | bytes 73732
  83.1 6.1 %copy-start.18 = (f32[12,512]{1,0:T(8,128)}, f32[12,512]{1,0:T(8,128)S(1)}, u32[]{:S(2)}) copy-start(f32[12,512]{1,0:T(8,128)S(1)} %fusion) | copy-start | bytes 73732
  84.1 5.1 %copy-start.5 = (bf16[512,768]{1,0:T(8,128)(2,1)S(1)}, bf16[512,768]{1,0:T(8,128)(2,1)}, u32[]{:S(2)}) copy-start(bf16[512,768]{1,0:T(8,128)(2,1)} %param.14) | copy-start | bytes 2359300
  84.1 5.2 %copy-start.38 = (bf16[768,768]{1,0:T(8,128)(2,1)S(1)}, bf16[768,768]{1,0:T(8,128)(2,1)}, u32[]{:S(2)}) copy-start(bf16[768,768]{1,0:T(8,128)(2,1)} %param.22) | copy-start | bytes 3538948
  193.1 4.6 %copy-start.36 = (s32[10]{0:T(128)S(1)}, s32[10]{0:T(128)}, u32[]{:S(2)}) copy-start(s32[10]{0:T(128)} %get-tuple-element.25) | copy-start | bytes 124
  193.1 43.2 %all-to-all-start.1 = ((bf16[8,128,768]{2,1,0:T(8,128)(2,1)}), bf16[8,128,768]{2,1,0:T(8,128)(2,1)}, u32[]{:S(2)}, u32[]{:S(2)}) async-start(bf16[8,128,768]{2,1,0:T(8,128)(2,1)} %slice.64), calls=%async_computation.1 | async-start | bytes 3145728 | tf_op jit(solution)/shard_map/all_to_all | solution.py:495
  222.4 3.1 copy-start.27
  251.6 16.6 %copy-start.3 = (f32[512,768]{1,0:T(8,128)S(1)}, f32[512,768]{1,0:T(8,128)}, u32[]{:S(2)}) copy-start(f32[512,768]{1,0:T(8,128)} %copy-done.2) | copy-start | bytes 4718596
  251.6 16.7 %copy-start.4 = (f32[512,768]{1,0:T(8,128)S(1)}, f32[512,768]{1,0:T(8,128)}, u32[]{:S(2)}) copy-start(f32[512,768]{1,0:T(8,128)} %reduce_sum.185) | copy-start | bytes 4718596
  251.6 16.7 %copy-start.21 = (f32[512]{0:T(512)S(1)}, f32[512]{0:T(512)}, u32[]{:S(2)}) copy-start(f32[512]{0:T(512)} %copy-done.20) | copy-start | bytes 6148
  251.6 16.7 %copy-start.33 = (f32[512]{0:T(512)S(1)}, f32[512]{0:T(512)}, u32[]{:S(2)}) copy-start(f32[512]{0:T(512)} %multiply_multiply_fusion.1) | copy-start | bytes 6148
  275.0 13.5 %slice-start = ((s8[12582912]{0:T(1024)(128)(4,1)}), s8[4194304]{0:T(1024)(128)(4,1)S(1)}, s32[]{:S(2)}) async-start(s8[12582912]{0:T(1024)(128)(4,1)} %bitcast.74), calls=%async_computation.5 | async-start | bytes 8388608
  275.0 13.5 %slice-start.1 = ((s8[12582912]{0:T(1024)(128)(4,1)}), s8[4194304]{0:T(1024)(128)(4,1)S(1)}, s32[]{:S(2)}) async-start(s8[12582912]{0:T(1024)(128)(4,1)} %bitcast.74), calls=%async_computation.6 | async-start | bytes 8388608
  275.0 13.5 %slice-start.2 = ((s8[12582912]{0:T(1024)(128)(4,1)}), s8[4194304]{0:T(1024)(128)(4,1)S(1)}, s32[]{:S(2)}) async-start(s8[12582912]{0:T(1024)(128)(4,1)} %bitcast.74), calls=%async_computation.7 | async-start | bytes 8388608
  275.0 13.5 %copy-start.10 = (pred[512,512]{0,1:T(8,128)(4,1)S(1)}, pred[512,512]{0,1:T(8,128)(4,1)}, u32[]{:S(2)}) copy-start(pred[512,512]{0,1:T(8,128)(4,1)} %copy-done.9) | copy-start | bytes 786436
  275.0 13.5 %copy-start.17 = (f32[12,512]{1,0:T(8,128)S(1)}, f32[12,512]{1,0:T(8,128)}, u32[]{:S(2)}) copy-start(f32[12,512]{1,0:T(8,128)} %log_add_fusion) | copy-start | bytes 73732
  288.6 7.3 %copy-start.8 = (bf16[512,768]{0,1:T(8,128)(2,1)S(1)}, bf16[512,768]{0,1:T(8,128)(2,1)}, u32[]{:S(2)}) copy-start(bf16[512,768]{0,1:T(8,128)(2,1)} %copy.60) | copy-start | bytes 2359300
  299.1 4.1 %copy-start.6 = (bf16[512,768]{1,0:T(8,128)(2,1)S(1)}, bf16[512,768]{1,0:T(8,128)(2,1)}, u32[]{:S(2)}) copy-start(bf16[512,768]{1,0:T(8,128)(2,1)} %param.14) | copy-start | bytes 2359300
  299.1 4.1 copy-start.30
  303.2 3.2 copy-start.42
  (20 other events, 35.6 us)
Sparse Core Ops, SparseCore 0:
  9.6 40.1 all-gather.1
  190.6 77.5 reduce-scatter.1
where the time goes:
time: 416 us; the launch traced here: 408 us
  Pallas kernels  158 us (38%)
  local copies, waits for them, and re-layouts  94.5 us (23%)
  other arithmetic  77.2 us (19%)
  matrix products  39.9 us (10%)
  between operations  15.2 us (4%)
  starting transfers between devices  12.4 us (3%)
  waiting for transfers between devices  10.9 us (3%)
    pallas_call x1, Pallas kernels, experts(): pl.pallas_call(functools.partial(expert_kernel, dp_size, ex_size, cap), o...  84.9 us
    pallas_call x1, Pallas kernels, all_reduce(): pl.pallas_call(functools.partial(reduce_kernel, dp_size, ex_size), out_sh...  73 us
    reduce_sum x1, other arithmetic, body(): output = mixed_rows + jnp.sum(picked * gates[:, :, None], axis=1)  16.6 us
    dot_general x1, matrix products, body(): jnp.einsum('qhd,khd->hqk', attended_heads, value_heads, preferred_element...  13.5 us
    all_to_all x1, waiting for transfers between devices, body(): lax.all_to_all(served[FROZEN:], 'expert', split_axis=0, concat_axis=0, ti...  10.2 us
  transfers between devices with their start and end apart: 4, of which 1 were waited for; matrix products, arithmetic and copies ran while one was open for 49% of the time, Pallas kernels for 18%

commit v1 on v0

v1 whole, which is shorter than its diff:
```python
import functools
import jax
import jax.numpy as jnp
from jax import lax
from jax.experimental import pallas as pl
from jax.experimental.pallas import tpu as pltpu
from jax.sharding import PartitionSpec as P

MESH = pl.DeviceIdType.MESH


def butterfly(dp_size, ex_size):
    core = ("dp", 1)
    xs = [("dp", 2 << k) for k in range((dp_size // 2).bit_length() - 1)]
    depth = 4 if ex_size % 4 == 0 else 1
    wide = ex_size // depth
    ys = [("expert", 1 << k) for k in range(wide.bit_length() - 1)]
    zs = [("expert", wide << k) for k in range(depth.bit_length() - 1)]
    return core, xs, ys, zs


def partner_of(step):
    axis, mask = step
    place = {"dp": lax.axis_index("dp"), "expert": lax.axis_index("expert")}
    bit = lax.rem(place[axis] // mask, 2)
    place[axis] = place[axis] + mask - 2 * mask * bit
    return bit, (place["dp"], place["expert"])


def dot_nn(a, b):
    return jnp.dot(a, b, preferred_element_type=jnp.float32)


def dot_nt(a, b):
    return lax.dot_general(a, b, (((1,), (1,)), ((), ())), preferred_element_type=jnp.float32)


def dot_tn(a, b):
    return lax.dot_general(a, b, (((0,), (0,)), ((), ())), preferred_element_type=jnp.float32)


GELU_A = 0.7978845608028654
GELU_B = GELU_A * 0.044715


def gelu_pair(h):
    square = h * h
    bend = jnp.tanh(h * (GELU_B * square + GELU_A))
    share = 0.5 * bend + 0.5
    slope = share + (0.5 * h) * (1.0 - bend * bend) * ((3.0 * GELU_B) * square + GELU_A)
    return h * share, slope


def expert_kernel(dp_size, ex_size, cap, rows_hbm, fgrad_hbm, agrad_hbm, win_hbm, shard_hbm, fin_hbm, fout_hbm,
                  back_hbm, res_hbm, dw_hbm,
                  rows_v, grad_v, win_v, wout_v, act_v, hg_v, fin_v, fout_v, frow_v, fgrad_v, facc_v, fout_st,
                  rg_v, dw_st, send_row, recv_row, send_back, recv_back, send_w, recv_w, fwd_w, got_w,
                  load_sem, frozen_sem, fload_sem, store_sem, dw_sem):
    dp = lax.axis_index("dp")
    ex = lax.axis_index("expert")
    shard = shard_hbm.shape[0]
    feat = shard_hbm.shape[1]
    slots = ex_size * cap
    far = dp_size // 2
    tiles = win_hbm.shape[0] // 256
    span = fin_v.shape[1]
    steps = fin_hbm.shape[0]

    barrier = pltpu.get_barrier_semaphore()
    for r in range(1, ex_size):
        pl.semaphore_signal(barrier, inc=1, device_id=(dp, ex ^ r), device_id_type=MESH)
    pl.semaphore_signal(barrier, inc=1, device_id=(dp ^ 1, ex), device_id_type=MESH)
    for k in range(1, far):
        pl.semaphore_signal(barrier, inc=1, device_id=(dp ^ (2 * k), ex), device_id_type=MESH)
    local = [
        pltpu.make_async_copy(rows_hbm.at[pl.ds(0, 2)], frow_v, load_sem.at[0]),
        pltpu.make_async_copy(fgrad_hbm, fgrad_v, load_sem.at[1]),
    ]
    for copy in local:
        copy.start()

    def frozen_load(i, slot):
        return (pltpu.make_async_copy(fin_hbm.at[i], fin_v.at[slot], frozen_sem.at[0, slot]),
                pltpu.make_async_copy(fout_hbm.at[i], fout_v.at[slot], frozen_sem.at[1, slot]))

    for copy in frozen_load(0, 0):
        copy.start()
    pl.semaphore_wait(barrier, ex_size - 1 + 1 + far - 1)

    row_copies = []
    for r in reversed(range(1, ex_size)):
        copy = pltpu.make_async_remote_copy(
            src_ref=rows_hbm.at[2 + (ex ^ r)], dst_ref=rows_v.at[pl.ds(r * cap, cap)],
            send_sem=send_row.at[r], recv_sem=recv_row.at[r], device_id=(dp, ex ^ r), device_id_type=MESH)
        copy.start()
        row_copies.append(copy)
    own = [pltpu.make_async_copy(rows_hbm.at[2 + ex], rows_v.at[pl.ds(0, cap)], load_sem.at[2]),
           pltpu.make_async_copy(win_hbm, win_v, load_sem.at[3]),
           pltpu.make_async_copy(shard_hbm, wout_v.at[pl.ds(pl.multiple_of(dp * shard, shard), shard)], load_sem.at[4])]
    for copy in own:
        copy.start()

    mine = wout_v.at[pl.ds(pl.multiple_of(dp * shard, shard), shard)]
    weight_copies = []
    for k in range(1, far):
        copy = pltpu.make_async_remote_copy(
            src_ref=shard_hbm, dst_ref=mine, send_sem=send_w.at[k], recv_sem=recv_w.at[k],
            device_id=(dp ^ (2 * k), ex), device_id_type=MESH)
        copy.start()
        weight_copies.append(copy)
    beside = pltpu.make_async_remote_copy(
        src_ref=shard_hbm, dst_ref=mine, send_sem=send_w.at[0], recv_sem=recv_w.at[0],
        device_id=(dp ^ 1, ex), device_id_type=MESH)
    beside.start()
    grad_copies = []
    for r in range(ex_size):
        copy = pltpu.make_async_copy(agrad_hbm.at[ex ^ r], grad_v.at[pl.ds(r * cap, cap)], fload_sem.at[r])
        copy.start()
        grad_copies.append(copy)

    for copy in local:
        copy.wait()
    per = steps // 2

    def frozen(i, _):
        slot = lax.rem(i, 2)
        for copy in frozen_load(i, slot):
            copy.wait()

        @pl.when(i + 1 < steps)
        def _():
            for copy in frozen_load(i + 1, 1 - slot):
                copy.start()
        which = i // per
        up = fin_v[slot]
        down = fout_v[slot]
        hidden = dot_nt(frow_v[which], up)
        slope_in = dot_nt(fgrad_v[which], down)
        active, slope = gelu_pair(hidden)
        result = dot_nn(active.astype(jnp.bfloat16), down)
        back = dot_nn((slope_in * slope).astype(jnp.bfloat16), up)
        first = lax.rem(i, per) == 0

        @pl.when(first)
        def _():
            facc_v[0, which] = result
            facc_v[1, which] = back

        @pl.when(jnp.logical_not(first))
        def _():
            facc_v[0, which] += result
            facc_v[1, which] += back
        return 0

    lax.fori_loop(0, steps, frozen, 0)
    fout_st[...] = facc_v[...].astype(jnp.bfloat16)
    stores = [pltpu.make_async_copy(fout_st.at[0], res_hbm.at[pl.ds(0, 2)], store_sem.at[0]),
              pltpu.make_async_copy(fout_st.at[1], back_hbm.at[pl.ds(0, 2)], store_sem.at[1])]
    for copy in stores:
        copy.start()

    passed = []
    for k in range(1, far):
        weight_copies[k - 1].wait_recv()
        theirs = wout_v.at[pl.ds(pl.multiple_of((dp ^ (2 * k)) * shard, shard), shard)]
        copy = pltpu.make_async_remote_copy(
            src_ref=theirs, dst_ref=theirs, send_sem=fwd_w.at[k], recv_sem=got_w.at[k],
            device_id=(dp ^ 1, ex), device_id_type=MESH)
        copy.start()
        passed.append(copy)
    beside.wait_recv()
    for copy in passed:
        copy.wait_recv()
    for copy in grad_copies:
        copy.wait()
    for copy in own:
        copy.wait()

    def slope_tile(t, _):
        at = pl.ds(pl.multiple_of(t * 256, 256), 256)
        hg_v[:, at] = dot_nt(grad_v[...], wout_v[at, :]).astype(jnp.bfloat16)
        return 0

    lax.fori_loop(0, tiles, slope_tile, 0)
    back_copies = []
    half = slots // 2
    for part in (1, 0):
        here = pl.ds(part * half, half)
        group = range(part * (ex_size // 2), (part + 1) * (ex_size // 2))
        for r in group:
            if r:
                row_copies[ex_size - 1 - r].wait_recv()

        def hidden_tile(t, _, here=here):
            at = pl.ds(pl.multiple_of(t * 256, 256), 256)
            active, slope = gelu_pair(dot_nt(rows_v[here, :], win_v[at, :]))
            act_v[here, at] = active.astype(jnp.bfloat16)
            hg_v[here, at] = (hg_v[here, at].astype(jnp.float32) * slope).astype(jnp.bfloat16)
            return 0

        lax.fori_loop(0, tiles, hidden_tile, 0)

        def back_tile(n, _, here=here):
            at = pl.ds(pl.multiple_of(n * 256, 256), 256)
            rg_v[here, at] = dot_nn(hg_v[here, :], win_v[:, at]).astype(jnp.bfloat16)
            return 0

        lax.fori_loop(0, feat // 256, back_tile, 0)
        for r in reversed(group):
            source = rg_v.at[pl.ds(r * cap, cap)]
            if r:
                copy = pltpu.make_async_remote_copy(
                    src_ref=source, dst_ref=back_hbm.at[2 + ex], send_sem=send_back.at[r], recv_sem=recv_back.at[r],
                    device_id=(dp, ex ^ r), device_id_type=MESH)
            else:
                copy = pltpu.make_async_copy(source, back_hbm.at[2 + ex], store_sem.at[2])
            copy.start()
            back_copies.append(copy)

    def result_tile(n, _):
        at = pl.ds(pl.multiple_of(n * 256, 256), 256)
        grad_st[:, at] = dot_nn(act_v[...], wout_v[:, at]).astype(jnp.bfloat16)
        return 0

    def weight_tile(t, _):
        at = pl.ds(pl.multiple_of(t * 256, 256), 256)
        slot = lax.rem(t, 2)

        @pl.when(t >= 2)
        def _():
            pltpu.make_async_copy(dw_st.at[slot], dw_hbm.at[at], dw_sem.at[slot]).wait()
        dw_st[slot, :, 0:feat] = dot_tn(hg_v[:, at], rows_v[...]).astype(jnp.bfloat16)
        dw_st[slot, :, feat:] = dot_tn(act_v[:, at], grad_v[...]).astype(jnp.bfloat16)
        pltpu.make_async_copy(dw_st.at[slot], dw_hbm.at[at], dw_sem.at[slot]).start()
        return 0

    lax.fori_loop(0, tiles, weight_tile, 0)
    grad_st = grad_v
    lax.fori_loop(0, feat // 256, result_tile, 0)
    res_copies = []
    for r in range(ex_size):
        copy = pltpu.make_async_copy(grad_st.at[pl.ds(r * cap, cap)], res_hbm.at[2 + (ex ^ r)], fload_sem.at[r])
        copy.start()
        res_copies.append(copy)
    for slot in range(2):
        pltpu.make_async_copy(dw_st.at[slot], dw_hbm.at[pl.ds(0, 256)], dw_sem.at[slot]).wait()
    for copy in res_copies + stores:
        copy.wait()
    for copy in weight_copies:
        copy.wait_send()
    beside.wait_send()
    for copy in passed:
        copy.wait_send()
    for copy in row_copies:
        copy.wait_send()
    for copy in back_copies:
        copy.wait()


def experts(rows, fgrad, agrad, win, shard, fin, fout, dp_size, ex_size):
    kinds, cap, feat = rows.shape
    hidden = win.shape[0]
    slots = ex_size * cap
    far = dp_size // 2
    span = 768 if hidden % 768 == 0 else hidden
    steps = 2 * hidden // span
    anyspace = pl.BlockSpec(memory_space=pl.ANY)
    dma = pltpu.SemaphoreType.DMA
    low = jnp.bfloat16
    return pl.pallas_call(
        functools.partial(expert_kernel, dp_size, ex_size, cap),
        out_shape=(jax.ShapeDtypeStruct((kinds, cap, feat), low), jax.ShapeDtypeStruct((kinds, cap, feat), low),
                   jax.ShapeDtypeStruct((hidden, 2 * feat), low)),
        in_specs=[anyspace] * 7,
        out_specs=(anyspace,) * 3,
        scratch_shapes=[
            pltpu.VMEM((slots, feat), low), pltpu.VMEM((slots, feat), low),
            pltpu.VMEM((hidden, feat), low), pltpu.VMEM((hidden, feat), low),
            pltpu.VMEM((slots, hidden), low), pltpu.VMEM((slots, hidden), low),
            pltpu.VMEM((2, span, feat), low), pltpu.VMEM((2, span, feat), low),
            pltpu.VMEM((2, cap, feat), low), pltpu.VMEM((2, cap, feat), low),
            pltpu.VMEM((2, 2, cap, feat), jnp.float32), pltpu.VMEM((2, 2, cap, feat), low),
            pltpu.VMEM((slots, feat), low), pltpu.VMEM((2, 256, 2 * feat), low),
            dma((ex_size,)), dma((ex_size,)), dma((ex_size,)), dma((ex_size,)),
            dma((far,)), dma((far,)), dma((far,)), dma((far,)),
            dma((5,)), dma((2, 2)), dma((ex_size,)), dma((3,)), dma((2,)),
        ],
        compiler_params=pltpu.CompilerParams(collective_id=1, has_side_effects=True, vmem_limit_bytes=60 << 20),
        name="experts",
    )(rows, fgrad, agrad, win, shard, fin.reshape(steps, span, feat), fout.reshape(steps, span, feat))


def attend_kernel(dp_size, ex_size, kinds, cap, lengths_s, chosen_ref, gates_ref, keep_ref, tok_ref, cot_ref, gain1_ref,
                  gain2_ref, wqkv_hbm, wo_hbm, shard_hbm,
                  rows_hbm, fgrad_hbm, agrad_hbm, win_hbm, proj_hbm, prob_hbm, attt_hbm, normt_hbm, mixed_ref, place_ref,
                  count_ref,
                  wqkv_v, wo_v, norm_v, normt_v, proj_v, prob_v, attt_v, att_v, bias_v, grad_v, rows_v, place_v,
                  send_g, recv_g, send_w, recv_w, fwd_w, got_w, load_sem, store_sem, prob_sem):
    dp = lax.axis_index("dp")
    ex = lax.axis_index("expert")
    count, feat = tok_ref.shape
    shard = shard_hbm.shape[0]
    far = dp_size // 2
    low = jnp.bfloat16

    barrier = pltpu.get_barrier_semaphore()
    for r in range(1, ex_size):
        pl.semaphore_signal(barrier, inc=1, device_id=(dp, ex ^ r), device_id_type=MESH)
    pl.semaphore_signal(barrier, inc=1, device_id=(dp ^ 1, ex), device_id_type=MESH)
    for k in range(1, far):
        pl.semaphore_signal(barrier, inc=1, device_id=(dp ^ (2 * k), ex), device_id_type=MESH)
    mine = win_hbm.at[pl.ds(pl.multiple_of(dp * shard, shard), shard)]
    loads = [pltpu.make_async_copy(wqkv_hbm, wqkv_v, load_sem.at[0]),
             pltpu.make_async_copy(wo_hbm, wo_v, load_sem.at[1]),
             pltpu.make_async_copy(shard_hbm, mine, load_sem.at[2])]
    for copy in loads:
        copy.start()

    kind = lax.broadcasted_iota(jnp.int32, (128, count), 0)
    first = chosen_ref[0:1, :]
    second = chosen_ref[1:2, :]
    hit_first = jnp.where(kind == first, 1.0, 0.0)
    hit_second = jnp.where(kind == second, 1.0, 0.0)
    hits = (hit_first + hit_second).astype(low)
    before = jnp.where(lax.broadcasted_iota(jnp.int32, (count, count), 0)
                       < lax.broadcasted_iota(jnp.int32, (count, count), 1), 1.0, 0.0).astype(low)
    ahead = dot_nn(hits, before)
    count_ref[...] = dot_nt(jnp.ones((8, count), low), hits)
    place_first = first.astype(jnp.float32) * cap + jnp.sum(hit_first * ahead, axis=0, keepdims=True)
    place_second = second.astype(jnp.float32) * cap + jnp.sum(hit_second * ahead, axis=0, keepdims=True)
    place_v[0:1, :] = place_first
    place_v[1:2, :] = place_second

    spot = lax.broadcasted_iota(jnp.int32, (1, count), 1)
    document = jnp.zeros((1, count), jnp.float32)
    end = lengths_s[0, 0]
    for j in range(1, lengths_s.shape[1] + 1):
        document = document + jnp.where(spot >= end, 1.0, 0.0)
        if j < lengths_s.shape[1]:
            end = end + lengths_s[0, j]
    place_v[2:3, :] = document
    place_v[3:4, :] = keep_ref[...].astype(jnp.float32)
    place_v[4:8, :] = jnp.zeros((4, count), jnp.float32)
    columns = place_v[...].T
    place_ref[...] = columns

    def chosen_rows(e):
        slot = (e * cap + lax.broadcasted_iota(jnp.int32, (cap, count), 0)).astype(jnp.float32)
        return slot == place_v[0:1, :], slot == place_v[1:2, :]

    def grad_rows(e, _):
        one, two = chosen_rows(e)
        gate = jnp.sum(jnp.where(one, gates_ref[0:1, :], jnp.where(two, gates_ref[1:2, :], 0.0)), axis=1, keepdims=True)
        pick = jnp.where(one | two, 1.0, 0.0).astype(low)
        grad_v[e] = (dot_nn(pick, cot_ref[...]) * gate).astype(low)
        return 0

    lax.fori_loop(0, kinds, grad_rows, 0)
    pl.semaphore_wait(barrier, ex_size - 1 + 1 + far - 1)
    grad_copies = []
    for r in reversed(range(1, ex_size)):
        copy = pltpu.make_async_remote_copy(
            src_ref=grad_v.at[2 + (ex ^ r)], dst_ref=agrad_hbm.at[ex],
            send_sem=send_g.at[r], recv_sem=recv_g.at[r], device_id=(dp, ex ^ r), device_id_type=MESH)
        copy.start()
        grad_copies.append(copy)
    weight_copies = []
    for k in range(1, far):
        copy = pltpu.make_async_remote_copy(
            src_ref=shard_hbm, dst_ref=mine, send_sem=send_w.at[k], recv_sem=recv_w.at[k],
            device_id=(dp ^ (2 * k), ex), device_id_type=MESH)
        copy.start()
        weight_copies.append(copy)
    beside = pltpu.make_async_remote_copy(
        src_ref=shard_hbm, dst_ref=mine, send_sem=send_w.at[0], recv_sem=recv_w.at[0],
        device_id=(dp ^ 1, ex), device_id_type=MESH)
    beside.start()
    stores = [pltpu.make_async_copy(grad_v.at[2 + ex], agrad_hbm.at[ex], store_sem.at[0]),
              pltpu.make_async_copy(grad_v.at[pl.ds(0, 2)], fgrad_hbm, store_sem.at[1])]
    for copy in stores:
        copy.start()

    whole = tok_ref[...].astype(jnp.float32)
    centred = whole - jnp.mean(whole, axis=1, keepdims=True)
    scale = lax.rsqrt(jnp.mean(centred * centred, axis=1, keepdims=True) + 1e-05)
    norm_v[...] = (centred * scale * gain1_ref[...][None]).astype(low)
    loads[0].wait()

    def project(n, _):
        at = pl.ds(pl.multiple_of(n * 256, 256), 256)
        proj_v[:, at] = dot_nn(norm_v[...], wqkv_v[:, at]).astype(low)
        return 0

    lax.fori_loop(0, 3 * feat // 256, project, 0)
    stores.append(pltpu.make_async_copy(proj_v, proj_hbm, store_sem.at[2]))
    stores[-1].start()

    key = lax.broadcasted_iota(jnp.int32, (count, count), 0)
    query = lax.broadcasted_iota(jnp.int32, (count, count), 1)
    allowed = (columns[:, 2:3] == document) & (key <= query) & ((columns[:, 3:4] > 0.0) | (key == query))
    bias_v[...] = jnp.where(allowed, 0.0, -1e30)
    half = count // 2
    lower = lax.broadcasted_iota(jnp.int32, (count, 128), 1) < 64

    def head_pair(p, _):
        at = pl.multiple_of(p * 128, 128)
        q = proj_v[:, pl.ds(at, 128)]
        k = proj_v[:, pl.ds(pl.multiple_of(feat + p * 128, 128), 128)]
        vt = proj_v[:, pl.ds(pl.multiple_of(2 * feat + p * 128, 128), 128)].T
        for j in range(2):
            one = jnp.where(lower if j == 0 else jnp.logical_not(lower), k, jnp.zeros_like(k))
            for b in range(2):
                reach = (b + 1) * half
                scores = dot_nt(one[0:reach], q[b * half:(b + 1) * half]) * 0.125 + bias_v[0:reach, b * half:(b + 1) * half]
                powers = jnp.exp(scores - jnp.max(scores, axis=0, keepdims=True))
                probs = (powers * (1.0 / jnp.sum(powers, axis=0, keepdims=True))).astype(low)
                prob_v[2 * p + j, b * half:b * half + reach, :] = probs
                attt_v[pl.ds(at + 64 * j, 64), b * half:(b + 1) * half] = dot_nn(
                    vt[64 * j:64 * j + 64, 0:reach], probs).astype(low)
        pltpu.make_async_copy(prob_v.at[pl.ds(2 * p, 2)], prob_hbm.at[pl.ds(2 * p, 2)], prob_sem.at[p]).start()
        return 0

    lax.fori_loop(0, feat // 128, head_pair, 0)
    stores.append(pltpu.make_async_copy(attt_v, attt_hbm, store_sem.at[3]))
    stores[-1].start()

    def turn(n, _):
        at = pl.ds(pl.multiple_of(n * 128, 128), 128)
        att_v[:, at] = attt_v[at, :].T
        return 0

    lax.fori_loop(0, feat // 128, turn, 0)
    loads[1].wait()

    def mix(n, _):
        at = pl.ds(pl.multiple_of(n * 256, 256), 256)
        mixed_ref[:, at] = tok_ref[:, at].astype(jnp.float32) + dot_nn(att_v[...], wo_v[:, at])
        return 0

    lax.fori_loop(0, feat // 256, mix, 0)
    mixed = mixed_ref[...]
    centred = mixed - jnp.mean(mixed, axis=1, keepdims=True)
    scale = lax.rsqrt(jnp.mean(centred * centred, axis=1, keepdims=True) + 1e-05)
    att_v[...] = (centred * scale * gain2_ref[...][None]).astype(low)

    def token_rows(e, _):
        one, two = chosen_rows(e)
        pick = jnp.where(one | two, 1.0, 0.0).astype(low)
        rows_v[e] = dot_nn(pick, att_v[...]).astype(low)
        return 0

    lax.fori_loop(0, kinds, token_rows, 0)
    stores.append(pltpu.make_async_copy(rows_v, rows_hbm, store_sem.at[4]))
    stores[-1].start()

    def turn_norm(n, _):
        at = pl.ds(pl.multiple_of(n * 128, 128), 128)
        normt_v[at, :] = norm_v[:, at].T
        return 0

    lax.fori_loop(0, feat // 128, turn_norm, 0)
    stores.append(pltpu.make_async_copy(normt_v, normt_hbm, store_sem.at[5]))
    stores[-1].start()

    passed = []
    for k in range(1, far):
        weight_copies[k - 1].wait_recv()
        theirs = win_hbm.at[pl.ds(pl.multiple_of((dp ^ (2 * k)) * shard, shard), shard)]
        copy = pltpu.make_async_remote_copy(
            src_ref=theirs, dst_ref=theirs, send_sem=fwd_w.at[k], recv_sem=got_w.at[k],
            device_id=(dp ^ 1, ex), device_id_type=MESH)
        copy.start()
        passed.append(copy)
    for p in range(feat // 128):
        pltpu.make_async_copy(prob_v.at[pl.ds(2 * p, 2)], prob_hbm.at[pl.ds(2 * p, 2)], prob_sem.at[p]).wait()
    for copy in stores:
        copy.wait()
    loads[2].wait()
    for copy in weight_copies:
        copy.wait_send()
    beside.wait()
    for copy in passed:
        copy.wait()
    for copy in grad_copies:
        copy.wait()


def attend(tokens, cotangent, chosen, gates, lengths, keep, gain1, gain2, wqkv, wo, shard, kinds, cap, dp_size, ex_size):
    count, feat = tokens.shape
    heads = feat // 64
    anyspace = pl.BlockSpec(memory_space=pl.ANY)
    vmem = pl.BlockSpec(memory_space=pltpu.VMEM)
    dma = pltpu.SemaphoreType.DMA
    low = jnp.bfloat16
    shape = jax.ShapeDtypeStruct
    far = dp_size // 2
    return pl.pallas_call(
        functools.partial(attend_kernel, dp_size, ex_size, kinds, cap),
        out_shape=(shape((kinds, cap, feat), low), shape((2, cap, feat), low), shape((ex_size, cap, feat), low),
                   shape((dp_size * shard.shape[0], feat), low), shape((count, 3 * feat), low),
                   shape((heads, count + count // 2, count // 2), low), shape((feat, count), low),
                   shape((feat, count), low), shape((count, feat), jnp.float32), shape((count, 8), jnp.float32),
                   shape((8, 128), jnp.float32)),
        in_specs=[pl.BlockSpec(memory_space=pltpu.SMEM)] + [vmem] * 7 + [anyspace] * 3,
        out_specs=(anyspace,) * 8 + (vmem,) * 3,
        scratch_shapes=[
            pltpu.VMEM((feat, 3 * feat), low), pltpu.VMEM((feat, feat), low), pltpu.VMEM((count, feat), low),
            pltpu.VMEM((feat, count), low), pltpu.VMEM((count, 3 * feat), low),
            pltpu.VMEM((heads, count + count // 2, count // 2), low), pltpu.VMEM((feat, count), low),
            pltpu.VMEM((count, feat), low), pltpu.VMEM((count, count), jnp.float32),
            pltpu.VMEM((kinds, cap, feat), low), pltpu.VMEM((kinds, cap, feat), low), pltpu.VMEM((8, count), jnp.float32),
            dma((ex_size,)), dma((ex_size,)), dma((far,)), dma((far,)), dma((far,)), dma((far,)),
            dma((3,)), dma((6,)), dma((feat // 128,)),
        ],
        compiler_params=pltpu.CompilerParams(collective_id=0, has_side_effects=True, vmem_limit_bytes=56 << 20),
        name="attend",
    )(lengths, chosen.T, gates.T, keep[None], tokens, cotangent, gain1, gain2, wqkv, wo, shard)


class Sums:

    def __init__(self, chunks, blocks, acc, got, out, ssem, rsem, gsem, hsem):
        self.chunks, self.blocks, self.acc, self.got, self.out = chunks, blocks, acc, got, out
        self.sems = (ssem, rsem, gsem, hsem)
        self.offs = [[base] for base, _, _, _ in chunks]
        self.land = [[base] for base, _, _, _ in chunks]
        self.copies = [None] * len(chunks)
        self.stage = [0] * len(chunks)
        self.sent = []

    def scatter(self, c, i):
        base, rows, order, _ = self.chunks[c]
        bit, peer = partner_of(order[i])
        half = rows >> (i + 1)
        source = self.blocks if i == 0 else self.acc
        give = pl.multiple_of(self.offs[c][i] + (1 - bit) * half, 16)
        copy = pltpu.make_async_remote_copy(
            src_ref=source.at[pl.ds(give, half)], dst_ref=self.got.at[pl.ds(self.land[c][i], half)],
            send_sem=self.sems[0].at[c, i], recv_sem=self.sems[1].at[c, i], device_id=peer, device_id_type=MESH)
        copy.start()
        self.offs[c].append(self.offs[c][i] + bit * half)
        self.land[c].append(self.land[c][i] + half)
        self.copies[c] = copy

    def gather(self, c, i):
        base, rows, order, _ = self.chunks[c]
        _, peer = partner_of(order[i])
        at = pl.ds(pl.multiple_of(self.offs[c][i + 1], 16), rows >> (i + 1))
        copy = pltpu.make_async_remote_copy(
            src_ref=self.out.at[at], dst_ref=self.out.at[at],
            send_sem=self.sems[2].at[c, i], recv_sem=self.sems[3].at[c, i], device_id=peer, device_id_type=MESH)
        copy.start()
        self.copies[c] = copy

    def start(self, phase):
        for c, chunk in enumerate(self.chunks):
            if chunk[3] == phase:
                self.scatter(c, 0)

    def advance(self, c):
        if self.copies[c] is None:
            return
        base, rows, order, _ = self.chunks[c]
        steps, s = len(order), self.stage[c]
        self.copies[c].wait()
        self.stage[c] += 1
        if s >= steps:
            i = 2 * steps - 1 - s
            if i > 0:
                self.gather(c, i - 1)
            else:
                self.copies[c] = None
            return
        half = rows >> (s + 1)
        source = self.blocks if s == 0 else self.acc
        target = self.acc if s + 1 < steps else self.out
        keep, begin = self.offs[c][s + 1], self.land[c][s]
        tile = half
        while tile > 128 or half % tile or tile % 16:
            tile -= 16

        def add(j, _):
            at = pl.ds(pl.multiple_of(keep + j * tile, 16), tile)
            other = self.got[pl.ds(pl.multiple_of(begin + j * tile, 16), tile), :]
            target[at, :] = (source[at, :].astype(jnp.float32) + other.astype(jnp.float32)).astype(jnp.bfloat16)
            return 0

        lax.fori_loop(0, half // tile, add, 0)
        if s + 1 < steps:
            self.scatter(c, s + 1)
        else:
            self.gather(c, s)

    def tick(self):
        for c in range(len(self.chunks)):
            self.advance(c)

    def finish(self):
        while any(copy is not None for copy in self.copies):
            self.tick()


def sum_chunks(dp_size, ex_size, rows):
    core, xs, ys, zs = butterfly(dp_size, ex_size)
    yxz, yzx, xyz = [core] + ys + xs + zs, [core] + ys + zs + xs, [core] + xs + ys + zs
    if dp_size * ex_size * 16 <= 512:
        return [(0, 1536, yxz, 0), (1536, 2048, yzx, 1), (3584, 1024, xyz, 2), (4608, 1536, yxz, 2)]
    third = rows // 3
    return [(0, third, yxz, 2), (third, third, yzx, 2), (2 * third, third, xyz, 2)]


def unwind_kernel(dp_size, ex_size, kinds, cap, back_hbm, res_hbm, proj_hbm, prob_hbm, attt_hbm, normt_hbm, wqkv_hbm, wo_hbm,
                  mixed_ref, tok_ref, cot_ref, place_ref, gates_ref, count_ref, gain1_ref, gain2_ref,
                  out_ref, dtok_ref, total_ref, sum_ref,
                  back_v, ret_v, pick_v, other_v, g_v, mg_v, branch_v, da_v, dqt_v, proj_v, prob_v, attt_v, normt_v, wqkv_v,
                  wo_v, pg_v, blocks_v, acc_v, got_v, gain_v, small_v, send_res, recv_res, ssem, rsem, gsem, hsem, tsem, usem,
                  load_sem):
    dp = lax.axis_index("dp")
    ex = lax.axis_index("expert")
    count, feat = tok_ref.shape
    slots = kinds * cap
    padded = back_v.shape[0]
    low = jnp.bfloat16
    steps = (dp_size * ex_size).bit_length() - 1
    bits = dp_size.bit_length() - 1

    barrier = pltpu.get_barrier_semaphore()
    for r in range(1, ex_size):
        pl.semaphore_signal(barrier, inc=1, device_id=(dp, ex ^ r), device_id_type=MESH)
    for k in range(bits):
        pl.semaphore_signal(barrier, inc=1, device_id=(dp ^ (1 << k), ex), device_id_type=MESH)
    loads = [pltpu.make_async_copy(source, target, load_sem.at[i]) for i, (source, target) in enumerate([
        (back_hbm, back_v.at[pl.ds(0, slots)]), (attt_hbm, attt_v), (wo_hbm, wo_v), (prob_hbm, prob_v), (proj_hbm, proj_v),
        (normt_hbm, normt_v), (wqkv_hbm, wqkv_v)])]
    for copy in loads:
        copy.start()
    pl.semaphore_wait(barrier, ex_size - 1 + bits)
    results = []
    for r in reversed(range(1, ex_size)):
        copy = pltpu.make_async_remote_copy(
            src_ref=res_hbm.at[pl.ds(pl.multiple_of((2 + (ex ^ r)) * cap, 16), cap)],
            dst_ref=ret_v.at[pl.ds(pl.multiple_of((2 + ex) * cap, 16), cap)],
            send_sem=send_res.at[r], recv_sem=recv_res.at[r], device_id=(dp, ex ^ r), device_id_type=MESH)
        copy.start()
        results.append(copy)
    own = pl.ds(pl.multiple_of((2 + ex) * cap, 16), cap)
    results.append(pltpu.make_async_copy(res_hbm.at[own], ret_v.at[own], load_sem.at[7]))
    results.append(pltpu.make_async_copy(res_hbm.at[pl.ds(0, 2 * cap)], ret_v.at[pl.ds(0, 2 * cap)], load_sem.at[8]))
    for copy in results[-2:]:
        copy.start()
    if padded > slots:
        ret_v[slots:, :] = jnp.zeros((padded - slots, feat), low)
        back_v[slots:, :] = jnp.zeros((padded - slots, feat), low)
    sums = Sums(sum_chunks(dp_size, ex_size, blocks_v.shape[0]), blocks_v, acc_v, got_v, total_ref, ssem, rsem, gsem, hsem)

    def place_tile(n):
        at = pl.ds(pl.multiple_of(n * 128, 128), 128)
        slot = (n * 128 + lax.broadcasted_iota(jnp.int32, (count, 128), 1)).astype(jnp.float32)
        return at, slot == place_ref[:, 0:1], slot == place_ref[:, 1:2]

    def pick_both(n, _):
        at, one, two = place_tile(n)
        pick_v[:, at] = jnp.where(one | two, 1.0, 0.0).astype(low)
        return 0

    lax.fori_loop(0, padded // 128, pick_both, 0)
    loads[0].wait()

    def collect(n, _):
        at = pl.ds(pl.multiple_of(n * 256, 256), 256)
        g_v[:, at] = dot_nn(pick_v[...], back_v[:, at])
        return 0

    lax.fori_loop(0, feat // 256, collect, 0)
    gain_v[...] = jnp.zeros_like(gain_v)
    gain_v[16:24, 0:128] = count_ref[...]

    def norm_back(i, whole, gain, target):
        at = pl.ds(pl.multiple_of(i * 64, 64), 64)
        centred = whole - jnp.mean(whole, axis=1, keepdims=True)
        scale = lax.rsqrt(jnp.mean(centred * centred, axis=1, keepdims=True) + 1e-05)
        unit = centred * scale
        grad = g_v[at, :]
        weighted = grad * unit
        gain_v[target:target + 8, :] += jnp.sum(weighted.reshape(8, 8, feat), axis=0)
        scaled = grad * gain
        return at, scale * (scaled - jnp.mean(scaled, axis=1, keepdims=True)
                            - unit * jnp.mean(scaled * unit, axis=1, keepdims=True))

    def second_norm(i, _):
        at, part = norm_back(i, mixed_ref[pl.ds(pl.multiple_of(i * 64, 64), 64), :], gain2_ref[...][None], 8)
        grad = cot_ref[at, :].astype(jnp.float32) + part
        mg_v[at, :] = grad
        branch_v[at, :] = grad.astype(low)
        return 0

    lax.fori_loop(0, count // 64, second_norm, 0)
    loads[1].wait()
    wide = feat // 2

    def out_weight(b, _):
        at = pl.ds(pl.multiple_of(b * wide, 128), wide)
        blocks_v[pl.ds(pl.multiple_of(b * feat, 16), feat), :] = dot_nn(attt_v[...], branch_v[:, at]).astype(low)
        return 0

    lax.fori_loop(0, 2, out_weight, 0)
    sums.start(0)
    loads[2].wait()

    def attended_grad(n, _):
        at = pl.ds(pl.multiple_of(n * 256, 256), 256)
        da_v[:, at] = dot_nt(branch_v[...], wo_v[at, :]).astype(low)
        return 0

    lax.fori_loop(0, feat // 256, attended_grad, 0)
    loads[3].wait()
    loads[4].wait()
    half = count // 2
    lower = lax.broadcasted_iota(jnp.int32, (count, 128), 1) < 64

    def head_pair(p, _):
        at_q = pl.ds(pl.multiple_of(p * 128, 128), 128)
        at_k = pl.ds(pl.multiple_of(feat + p * 128, 128), 128)
        at_v = pl.ds(pl.multiple_of(2 * feat + p * 128, 128), 128)
        q, k, v, da = proj_v[:, at_q], proj_v[:, at_k], proj_v[:, at_v], da_v[:, at_q]
        kt = k.T
        key_near = key_far = value_near = value_far = 0.0
        for j in range(2):
            mask = lower if j == 0 else jnp.logical_not(lower)
            qj, vj, daj = [jnp.where(mask, w, jnp.zeros_like(w)) for w in (q, v, da)]
            for b in range(2):
                reach, here = (b + 1) * half, slice(b * half, (b + 1) * half)
                prob = prob_v[2 * p + j, b * half:b * half + reach, :]
                full = prob.astype(jnp.float32)
                grad = dot_nt(vj[0:reach], da[here])
                score = (full * (grad - jnp.sum(full * grad, axis=0, keepdims=True))).astype(low)
                dqt_v[64 * j:64 * j + 64, here] = dot_nn(kt[64 * j:64 * j + 64, 0:reach], score)
                key_near += dot_nn(score[0:half], qj[here])
                value_near += dot_nn(prob[0:half], daj[here])
                if b:
                    key_far += dot_nn(score[half:], qj[here])
                    value_far += dot_nn(prob[half:], daj[here])
        pg_v[:, at_q] = (dqt_v[...].T * 0.125).astype(low)
        pg_v[0:half, at_k] = (key_near * 0.125).astype(low)
        pg_v[half:, at_k] = (key_far * 0.125).astype(low)
        pg_v[0:half, at_v] = value_near.astype(low)
        pg_v[half:, at_v] = value_far.astype(low)
        return 0

    pairs = feat // 128
    for turn in range(2):
        lax.fori_loop(turn * pairs // 2, (turn + 1) * pairs // 2, head_pair, 0)
        if turn == 0:
            loads[5].wait()
        sums.tick()

        def weight_block(c, _, turn=turn):
            at = pl.ds(pl.multiple_of(c * feat + turn * wide, 128), wide)
            into = pl.ds(pl.multiple_of(2 * feat + (3 * turn + c) * feat, 16), feat)
            blocks_v[into, :] = dot_nn(normt_v[...], pg_v[:, at]).astype(low)
            return 0

        lax.fori_loop(0, 3, weight_block, 0)
        sums.start(1 + turn)
    loads[6].wait()
    sums.tick()

    def norm_grad(n, _):
        at = pl.ds(pl.multiple_of(n * 256, 256), 256)
        g_v[:, at] = dot_nt(pg_v[...], wqkv_v[at, :])
        return 0

    lax.fori_loop(0, feat // 256, norm_grad, 0)
    sums.tick()

    def first_norm(i, _):
        here = pl.ds(pl.multiple_of(i * 64, 64), 64)
        at, part = norm_back(i, tok_ref[here, :].astype(jnp.float32), gain1_ref[...][None], 0)
        dtok_ref[at, :] = (mg_v[at, :] + part).astype(low)
        return 0

    lax.fori_loop(0, count // 64, first_norm, 0)
    for i in range(3):
        small_v[steps, i:i + 1, :] = jnp.sum(gain_v[8 * i:8 * i + 8, :], axis=0, keepdims=True)
    small_v[steps, 2:3, :] = gain_v[16:17, :]
    small_v[steps, 3:8, :] = jnp.zeros((5, feat), jnp.float32)
    order = sums.chunks[0][2]

    def small_send(i):
        _, peer = partner_of(order[i])
        copy = pltpu.make_async_remote_copy(
            src_ref=small_v.at[steps + i], dst_ref=small_v.at[i], send_sem=tsem.at[i], recv_sem=usem.at[i],
            device_id=peer, device_id_type=MESH)
        copy.start()
        return copy

    def small_add(i, copy):
        copy.wait()
        total = small_v[steps + i] + small_v[i]
        if i + 1 < steps:
            small_v[steps + i + 1] = total
            return small_send(i + 1)
        sum_ref[...] = total

    tiny = small_send(0)
    sums.tick()
    for copy in results:
        copy.wait()

    def pick_each(n, _):
        at, one, two = place_tile(n)
        pick_v[:, at] = jnp.where(one, 1.0, 0.0).astype(low)
        other_v[:, at] = jnp.where(two, 1.0, 0.0).astype(low)
        return 0

    lax.fori_loop(0, padded // 128, pick_each, 0)

    def deliver(n, _):
        at = pl.ds(pl.multiple_of(n * 256, 256), 256)
        one = dot_nn(pick_v[...], ret_v[:, at]) * gates_ref[:, 0:1]
        two = dot_nn(other_v[...], ret_v[:, at]) * gates_ref[:, 1:2]
        out_ref[:, at] = (mixed_ref[:, at] + (one + two)).astype(low)
        return 0

    lax.fori_loop(0, feat // 256, deliver, 0)
    for i in range(steps):
        sums.tick()
        tiny = small_add(i, tiny)
    sums.finish()


def unwind(back, res, proj, prob, attt, normt, wqkv, wo, mixed, tokens, cotangent, place, gates, tally, gain1, gain2,
           dp_size, ex_size):
    kinds, cap, feat = back.shape
    count = tokens.shape[0]
    slots = kinds * cap
    padded = (slots + 127) // 128 * 128
    heads = feat // 64
    steps = (dp_size * ex_size).bit_length() - 1
    rows, wide = 8 * feat, feat // 2
    anyspace = pl.BlockSpec(memory_space=pl.ANY)
    vmem = pl.BlockSpec(memory_space=pltpu.VMEM)
    dma = pltpu.SemaphoreType.DMA
    low, full = jnp.bfloat16, jnp.float32
    shape = jax.ShapeDtypeStruct
    chunks = len(sum_chunks(dp_size, ex_size, rows))
    return pl.pallas_call(
        functools.partial(unwind_kernel, dp_size, ex_size, kinds, cap),
        out_shape=(shape((count, feat), low), shape((count, feat), low), shape((rows, wide), low), shape((8, feat), full)),
        in_specs=[anyspace] * 8 + [vmem] * 8,
        out_specs=(vmem,) * 4,
        scratch_shapes=[
            pltpu.VMEM((padded, feat), low), pltpu.VMEM((padded, feat), low), pltpu.VMEM((count, padded), low),
            pltpu.VMEM((count, padded), low), pltpu.VMEM((count, feat), full), pltpu.VMEM((count, feat), full),
            pltpu.VMEM((count, feat), low), pltpu.VMEM((count, feat), low), pltpu.VMEM((128, count), full),
            pltpu.VMEM((count, 3 * feat), low), pltpu.VMEM((heads, count + count // 2, count // 2), low),
            pltpu.VMEM((feat, count), low), pltpu.VMEM((feat, count), low), pltpu.VMEM((feat, 3 * feat), low),
            pltpu.VMEM((feat, feat), low), pltpu.VMEM((count, 3 * feat), low), pltpu.VMEM((rows, wide), low),
            pltpu.VMEM((rows, wide), low), pltpu.VMEM((rows, wide), low), pltpu.VMEM((24, feat), full),
            pltpu.VMEM((2 * steps, 8, feat), full),
            dma((ex_size,)), dma((ex_size,)), dma((chunks, steps)), dma((chunks, steps)), dma((chunks, steps)),
            dma((chunks, steps)), dma((steps,)), dma((steps,)), dma((9,)),
        ],
        compiler_params=pltpu.CompilerParams(collective_id=2, has_side_effects=True, vmem_limit_bytes=62 << 20),
        name="unwind",
    )(back.reshape(slots, feat), res.reshape(slots, feat), proj, prob, attt, normt, wqkv, wo, mixed, tokens, cotangent,
      place, gates, tally, gain1, gain2)


FROZEN = 2


def body(
    tokens,
    cotangent,
    chosen,
    gates,
    lengths,
    keep_mask,
    gain1,
    w_qkv,
    w_o,
    gain2,
    frozen_in,
    frozen_out,
    w_in,
    w_out,
):
    row_count, feat_width = tokens.shape
    owners = lax.axis_size("expert")
    dp_size = lax.axis_size("dp")
    kind_count = FROZEN + owners
    slot_count = ((2 * row_count * 5 // (4 * kind_count) + 7) // 8 * 8 + 15) // 16 * 16
    rows, fgrad, agrad, weights_in, projected, probs_t, attended_t, norm_t, mixed_rows, place, tally = attend(
        tokens, cotangent, chosen, gates, lengths, keep_mask, gain1, gain2, w_qkv, w_o, w_in[0], kind_count, slot_count,
        dp_size, owners)
    row_grads, served, weight_grads = experts(
        rows, fgrad, agrad, weights_in, w_out[0], frozen_in, frozen_out, dp_size, owners)
    summed = lax.psum_scatter(weight_grads, "dp", scatter_dimension=0, tiled=True).astype(jnp.float32)
    d_w_in = summed[:, :feat_width][None]
    d_w_out = summed[:, feat_width:][None]
    output, tokens_grad, total, small_sum = unwind(
        row_grads, served, projected, probs_t, attended_t, norm_t, w_qkv, w_o, mixed_rows, tokens, cotangent, place, gates,
        tally, gain1, gain2, dp_size, owners)
    blocks = total.reshape(8, feat_width, feat_width // 2).astype(jnp.float32)
    w_o_sum = jnp.concatenate([blocks[0], blocks[1]], axis=1)
    w_qkv_sum = jnp.concatenate([blocks[i] for i in (2, 5, 3, 6, 4, 7)], axis=1)
    return (
        output,
        tokens_grad,
        small_sum[0],
        w_qkv_sum,
        w_o_sum,
        small_sum[1],
        d_w_in,
        d_w_out,
        small_sum[2, :kind_count],
    )


def solution(mesh):
    placed = (
        P(("dp", "expert"), None),
        P(("dp", "expert"), None),
        P(("dp", "expert"), None),
        P(("dp", "expert"), None),
        P(("dp", "expert"), None),
        P(("dp", "expert")),
        P(),
        P(),
        P(),
        P(),
        P(),
        P(),
        P("expert", "dp", None),
        P("expert", "dp", None),
    )
    return jax.shard_map(
        body,
        mesh=mesh,
        in_specs=placed,
        out_specs=(
            P(("dp", "expert"), None),
            P(("dp", "expert"), None),
            P(),
            P(),
            P(),
            P(),
            P("expert", "dp", None),
            P("expert", "dp", None),
            P(),
        ),
        check_vma=False,
    )
```

time: 416 us -> 283 us (0.68); the launches traced: 408 us -> 282 us
  Pallas kernels: 158 us -> 246 us
  local copies, waits for them, and re-layouts: 94.5 us -> 15.2 us
  other arithmetic: 77.2 us -> 6.98 us
  matrix products: 39.9 us -> 0 us
  starting transfers between devices: 12.4 us -> 0.04 us
  waiting for transfers between devices: 10.9 us -> 0.02 us
    pallas_call x1 -> x2, Pallas kernels: 73 us -> 161 us  [the longest x1 114 us: unwind(): pl.pallas_call(functools.partial(unwind_kernel, dp_size, ex_size, kinds,...]
    dot_general x12 -> x0, matrix products: 39.9 us -> none  [the longest x1 13.5 us: body(): jnp.einsum('qhd,khd->hqk', attended_heads, value_heads, preferred_element...]
    reduce_sum x11 -> x0, other arithmetic: 36.5 us -> none  [the longest x1 16.6 us: body(): output = mixed_rows + jnp.sum(picked * gates[:, :, None], axis=1)]
    slice x10 -> x1, local copies, waits for them, and re-layouts: 20.3 us -> 0.15 us  [body(): w_o_sum = jnp.concatenate([blocks[0], blocks[1]], axis=1)]
    gather x2 -> x0, local copies, waits for them, and re-layouts: 15.2 us -> none  [the longest x1 7.85 us: body(): row_grads[positions].astype(jnp.float32).reshape(row_count, 2, feat_width)]
    convert_element_type x4 -> x0, local copies, waits for them, and re-layouts: 14.7 us -> none  [the longest x1 4.86 us: body(): results[positions].astype(jnp.float32).reshape(row_count, 2, feat_width)]
    all_to_all x2 -> x0, starting transfers between devices: 12.2 us -> none  [the longest x1 7.53 us: body(): lax.all_to_all(grad_slots[FROZEN:], 'expert', split_axis=0, concat_axis=0...]
    convert_element_type x8 -> x2, other arithmetic: 17.2 us -> 5.39 us  [the longest x1 3.1 us: body(): blocks = total.reshape(8, feat_width, feat_width // 2).astype(jnp.float32)]
  transfers between devices with their start and end apart: 4 -> 1, of which waited for: 1 -> 0; matrix products, arithmetic and copies ran while one was open for 49% -> 5% of each run, Pallas kernels for 18% -> 41%
where the time goes in v1:
time: 283 us; the launch traced here: 282 us
  Pallas kernels  246 us (87%)
  local copies, waits for them, and re-layouts  15.2 us (5%)
  between operations  14.1 us (5%)
  other arithmetic  6.98 us (2%)
    pallas_call x1, Pallas kernels, unwind(): pl.pallas_call(functools.partial(unwind_kernel, dp_size, ex_size, kinds,...  114 us
    pallas_call x1, Pallas kernels, experts(): pl.pallas_call(functools.partial(expert_kernel, dp_size, ex_size, cap), o...  84.8 us
    pallas_call x1, Pallas kernels, attend(): pl.pallas_call(functools.partial(attend_kernel, dp_size, ex_size, kinds,...  46.5 us
    unnamed x16, local copies, waits for them, and re-layouts  8.73 us
  transfers between devices with their start and end apart: 1, of which 0 were waited for; matrix products, arithmetic and copies ran while one was open for 5% of the time, Pallas kernels for 41%

profile of v1, /device:TPU:0, one launch (start us, length us, event | category | flops | bytes accessed | tf_op | source)
XLA Modules:
  0.0 282.1 jit_solution(12147847215684461993)
XLA Ops:
  7.2 0.0 reduce-scatter.2.cloned.1.call-start
  7.2 46.5 %attend.1 = (bf16[10,128,768]{2,1,0:T(8,128)(2,1)}, bf16[2,128,768]{2,1,0:T(8,128)(2,1)}, bf16[8,128,768]{2,1,0:T(8,128)(2,1)}, bf16[3072,768]{1,0:T(8,128)(2,1)...) custom-call(s32[1,8]{1,0:T(1,128)} %lengths_s.1, ...), custom_call_target="tpu_custom_call" | custom-call | tf_op jit(solution)/shard_map/attend/pallas_call | solution.py:497
  53.8 84.8 %experts.1 = (bf16[10,128,768]{2,1,0:T(8,128)(2,1)}, bf16[10,128,768]{2,1,0:T(8,128)(2,1)}, bf16[3072,1536]{1,0:T(8,128)(2,1)}) custom-call(bf16[10,128,768]{2,1,0:T(8,128)(2,1)} %get-tuple-element.27.rows_hbm, bf16[2,128,768]{2,1,0:T(8,128)(2,1)} %get-tuple-element.28.fgrad_hbm, bf16[8,128,768]{2,1,0:T(8,128)(2,1)} %get-tuple-element.29.agrad_hbm, ...), custom_call_target="tpu_custom_call" | custom-call | tf_op jit(solution)/shard_map/experts/pallas_call | solution.py:270
  138.6 0.0 copy-start.3
  138.6 0.0 reduce-scatter.2.cloned.1.call-update
  138.7 0.7 copy-done.3
  139.3 0.9 copy.23.gates_ref
  140.2 114.4 %unwind.1 = (bf16[512,768]{1,0:T(8,128)(2,1)}, bf16[512,768]{1,0:T(8,128)(2,1)}, bf16[6144,384]{1,0:T(8,128)(2,1)}, f32[8,768]{1,0:T(8,128)}) custom-call(bf16[1280,768]{1,0:T(8,128)(2,1)} %bitcast.17, bf16[1280,768]{1,0:T(8,128)(2,1)} %bitcast.18, bf16[512,2304]{1,0:T(8,128)(2,1)} %get-tuple-element.33.proj_hbm, ...), custom_call_target="tpu_custom_call" | custom-call | tf_op jit(solution)/shard_map/unwind/pallas_call | solution.py:847
  254.5 0.0 copy-start
  254.6 3.1 %convert_element_type.7 = f32[6144,384]{1,0:T(8,128)S(1)} convert(bf16[6144,384]{1,0:T(8,128)(2,1)} %get-tuple-element.43) | non-fusion elementwise | flops 2359296 | bytes 14155776 | tf_op jit(solution)/shard_map/convert_element_type | solution.py:905
  257.7 1.4 slice_reduce_fusion
  259.1 0.0 copy-done
  259.1 0.2 fusion
  259.2 1.6 pad_maximum_fusion
  260.8 1.2 slice_bitcast_fusion.2
  262.0 1.1 slice_dynamic-update-slice_fusion.5
  263.1 1.1 slice_dynamic-update-slice_fusion.4
  264.2 1.1 slice_dynamic-update-slice_fusion.3
  265.3 1.1 slice_dynamic-update-slice_fusion.2
  266.4 1.1 slice_dynamic-update-slice_fusion.1
  267.5 1.1 slice_dynamic-update-slice_fusion
  268.6 0.0 reduce-scatter.2.cloned.1.call-done
  268.6 2.3 convert_element_type.8
  270.9 0.0 copy-start.2
  270.9 0.0 copy-start.1
  270.9 2.5 slice_bitcast_fusion
  273.4 0.0 copy-done.2
  273.4 0.9 copy.31
  274.3 0.0 copy-done.1
  274.3 0.9 copy.32
Async XLA Ops:
  7.2 261.4 %reduce-scatter.2.cloned.1.call-start = ((), (), s32[]{:S(2)}) async-start(), calls=%async_computation.1 | async-start | bytes 11796480 | tf_op jit(solution)/shard_map/reduce_scatter | solution.py:899
  138.6 0.7 copy-start.3
  254.5 4.5 %copy-start = (bf16[6144,384]{1,0:T(8,128)(2,1)S(1)}, bf16[6144,384]{1,0:T(8,128)(2,1)}, u32[]{:S(2)}) copy-start(bf16[6144,384]{1,0:T(8,128)(2,1)} %get-tuple-element.43) | copy-start | bytes 14155780
  270.9 2.6 copy-start.2
  270.9 3.4 %copy-start.1 = (bf16[512,768]{1,0:T(8,128)(2,1)S(1)}, bf16[512,768]{1,0:T(8,128)(2,1)}, u32[]{:S(2)}) copy-start(bf16[512,768]{1,0:T(8,128)(2,1)} %get-tuple-element.61) | copy-start | bytes 2359300
Sparse Core Ops, SparseCore 0:
  138.8 97.4 reduce-scatter.1

commit v2 on v1

--- a/solution.py
+++ b/solution.py
@@ -19,12 +19,17 @@
     return core, xs, ys, zs
 
 
-def partner_of(step):
-    axis, mask = step
+def group_of(stage):
     place = {"dp": lax.axis_index("dp"), "expert": lax.axis_index("expert")}
-    bit = lax.rem(place[axis] // mask, 2)
-    place[axis] = place[axis] + mask - 2 * mask * bit
-    return bit, (place["dp"], place["expert"])
+    mine = sum(lax.rem(place[axis] // mask, 2) << j for j, (axis, mask) in enumerate(stage))
+    peers = []
+    for m in range(1, 1 << len(stage)):
+        peer = dict(place)
+        for j, (axis, mask) in enumerate(stage):
+            if m >> j & 1:
+                peer[axis] = peer[axis] ^ mask
+        peers.append((peer["dp"], peer["expert"]))
+    return mine, peers
 
 
 def dot_nn(a, b):
@@ -51,11 +56,57 @@
     return h * share, slope
 
 
+class Scatter:
+
+    def __init__(self, dp, ex, far, core_v, pre_v, chip_v, sems):
+        self.dp, self.ex, self.far = dp, ex, far
+        self.core_v, self.pre_v, self.chip_v, self.sems = core_v, pre_v, chip_v, sems
+        self.cores, self.chips = {}, {}
+
+    def to_core(self, k, source):
+        self.cores[k] = pltpu.make_async_remote_copy(
+            src_ref=source, dst_ref=self.core_v.at[k], send_sem=self.sems[0].at[k], recv_sem=self.sems[1].at[k],
+            device_id=(self.dp ^ 1, self.ex), device_id_type=MESH)
+        self.cores[k].start()
+
+    def to_chip(self, k, source):
+        self.cores[k].wait_recv()
+
+        def add(j, _):
+            at = pl.ds(pl.multiple_of(j * 128, 128), 128)
+            total = source[at, :].astype(jnp.float32) + self.core_v[k, at, :].astype(jnp.float32)
+            self.pre_v[k, at, :] = total.astype(jnp.bfloat16)
+            return 0
+
+        lax.fori_loop(0, self.core_v.shape[1] // 128, add, 0)
+        self.chips[k] = pltpu.make_async_remote_copy(
+            src_ref=self.pre_v.at[k], dst_ref=self.chip_v.at[k], send_sem=self.sems[2].at[k], recv_sem=self.sems[3].at[k],
+            device_id=(self.dp ^ (2 * k), self.ex), device_id_type=MESH)
+        self.chips[k].start()
+
+    def total(self, source, target):
+        self.cores[0].wait_recv()
+        for k in range(1, self.far):
+            self.chips[k].wait_recv()
+
+        def add(j, _):
+            at = pl.ds(pl.multiple_of(j * 128, 128), 128)
+            total = source[at, :].astype(jnp.float32) + self.core_v[0, at, :].astype(jnp.float32)
+            for k in range(1, self.far):
+                total = total + self.chip_v[k, at, :].astype(jnp.float32)
+            target[at, :] = total
+            return 0
+
+        lax.fori_loop(0, self.core_v.shape[1] // 128, add, 0)
+        for copy in list(self.cores.values()) + list(self.chips.values()):
+            copy.wait_send()
+
+
 def expert_kernel(dp_size, ex_size, cap, rows_hbm, fgrad_hbm, agrad_hbm, win_hbm, shard_hbm, fin_hbm, fout_hbm,
-                  back_hbm, res_hbm, dw_hbm,
+                  back_hbm, res_hbm, dwo_hbm, dwin_ref,
                   rows_v, grad_v, win_v, wout_v, act_v, hg_v, fin_v, fout_v, frow_v, fgrad_v, facc_v, fout_st,
-                  rg_v, dw_st, send_row, recv_row, send_back, recv_back, send_w, recv_w, fwd_w, got_w,
-                  load_sem, frozen_sem, fload_sem, store_sem, dw_sem):
+                  rg_v, dwi_v, dwo_v, core_v, pre_v, chip_v, send_row, recv_row, send_back, recv_back, send_w, recv_w, fwd_w, got_w,
+                  load_sem, frozen_sem, fload_sem, store_sem, dw_sem, *scatter_sems):
     dp = lax.axis_index("dp")
     ex = lax.axis_index("expert")
     shard = shard_hbm.shape[0]
@@ -183,10 +234,10 @@
 
     lax.fori_loop(0, tiles, slope_tile, 0)
     back_copies = []
-    half = slots // 2
-    for part in (1, 0):
-        here = pl.ds(part * half, half)
-        group = range(part * (ex_size // 2), (part + 1) * (ex_size // 2))
+    whole = list(reversed(range(ex_size)))
+    groups = [whole[:ex_size // 4], whole[ex_size // 4:ex_size // 2], whole[ex_size // 2:]]
+    for group in groups:
+        here = pl.ds(group[-1] * cap, len(group) * cap)
         for r in group:
             if r:
                 row_copies[ex_size - 1 - r].wait_recv()
@@ -206,7 +257,7 @@
             return 0
 
         lax.fori_loop(0, feat // 256, back_tile, 0)
-        for r in reversed(group):
+        for r in group:
             source = rg_v.at[pl.ds(r * cap, cap)]
             if r:
                 copy = pltpu.make_async_remote_copy(
@@ -217,34 +268,49 @@
             copy.start()
             back_copies.append(copy)
 
+    width = 256 if shard % 256 == 0 else 128
+
+    def shard_at(which):
+        return pl.ds(pl.multiple_of(which * shard, shard), shard)
+
+    def in_shard(which):
+        def in_tile(j, _):
+            at = pl.ds(pl.multiple_of(which * shard + j * width, width), width)
+            dwi_v[at, :] = dot_tn(hg_v[:, at], rows_v[...]).astype(jnp.bfloat16)
+            return 0
+
+        lax.fori_loop(0, shard // width, in_tile, 0)
+
+    scatter = Scatter(dp, ex, far, core_v, pre_v, chip_v, scatter_sems)
+    for k in range(1, far):
+        in_shard(dp ^ (2 * k + 1))
+        scatter.to_core(k, dwi_v.at[shard_at(dp ^ (2 * k + 1))])
+        in_shard(dp ^ (2 * k))
+        scatter.to_chip(k, dwi_v.at[shard_at(dp ^ (2 * k))])
+    in_shard(dp ^ 1)
+    scatter.to_core(0, dwi_v.at[shard_at(dp ^ 1)])
+    in_shard(dp)
+
+    def out_tile(t, _):
+        at = pl.ds(pl.multiple_of(t * 256, 256), 256)
+        dwo_v[at, :] = dot_tn(act_v[:, at], grad_v[...]).astype(jnp.bfloat16)
+        return 0
+
+    lax.fori_loop(0, tiles, out_tile, 0)
+    stores.append(pltpu.make_async_copy(dwo_v, dwo_hbm, dw_sem.at[0]))
+    stores[-1].start()
+
     def result_tile(n, _):
         at = pl.ds(pl.multiple_of(n * 256, 256), 256)
-        grad_st[:, at] = dot_nn(act_v[...], wout_v[:, at]).astype(jnp.bfloat16)
-        return 0
-
-    def weight_tile(t, _):
-        at = pl.ds(pl.multiple_of(t * 256, 256), 256)
-        slot = lax.rem(t, 2)
-
-        @pl.when(t >= 2)
-        def _():
-            pltpu.make_async_copy(dw_st.at[slot], dw_hbm.at[at], dw_sem.at[slot]).wait()
-        dw_st[slot, :, 0:feat] = dot_tn(hg_v[:, at], rows_v[...]).astype(jnp.bfloat16)
-        dw_st[slot, :, feat:] = dot_tn(act_v[:, at], grad_v[...]).astype(jnp.bfloat16)
-        pltpu.make_async_copy(dw_st.at[slot], dw_hbm.at[at], dw_sem.at[slot]).start()
-        return 0
-
-    lax.fori_loop(0, tiles, weight_tile, 0)
-    grad_st = grad_v
+        grad_v[:, at] = dot_nn(act_v[...], wout_v[:, at]).astype(jnp.bfloat16)
+        return 0
+
     lax.fori_loop(0, feat // 256, result_tile, 0)
-    res_copies = []
     for r in range(ex_size):
-        copy = pltpu.make_async_copy(grad_st.at[pl.ds(r * cap, cap)], res_hbm.at[2 + (ex ^ r)], fload_sem.at[r])
-        copy.start()
-        res_copies.append(copy)
-    for slot in range(2):
-        pltpu.make_async_copy(dw_st.at[slot], dw_hbm.at[pl.ds(0, 256)], dw_sem.at[slot]).wait()
-    for copy in res_copies + stores:
+        stores.append(pltpu.make_async_copy(grad_v.at[pl.ds(r * cap, cap)], res_hbm.at[2 + (ex ^ r)], fload_sem.at[r]))
+        stores[-1].start()
+    scatter.total(dwi_v.at[shard_at(dp)], dwin_ref)
+    for copy in stores:
         copy.wait()
     for copy in weight_copies:
         copy.wait_send()
@@ -270,9 +336,9 @@
     return pl.pallas_call(
         functools.partial(expert_kernel, dp_size, ex_size, cap),
         out_shape=(jax.ShapeDtypeStruct((kinds, cap, feat), low), jax.ShapeDtypeStruct((kinds, cap, feat), low),
-                   jax.ShapeDtypeStruct((hidden, 2 * feat), low)),
+                   jax.ShapeDtypeStruct((hidden, feat), low), jax.ShapeDtypeStruct(shard.shape, jnp.float32)),
         in_specs=[anyspace] * 7,
-        out_specs=(anyspace,) * 3,
+        out_specs=(anyspace,) * 3 + (pl.BlockSpec(memory_space=pltpu.VMEM),),
         scratch_shapes=[
             pltpu.VMEM((slots, feat), low), pltpu.VMEM((slots, feat), low),
             pltpu.VMEM((hidden, feat), low), pltpu.VMEM((hidden, feat), low),
@@ -280,10 +346,12 @@
             pltpu.VMEM((2, span, feat), low), pltpu.VMEM((2, span, feat), low),
             pltpu.VMEM((2, cap, feat), low), pltpu.VMEM((2, cap, feat), low),
             pltpu.VMEM((2, 2, cap, feat), jnp.float32), pltpu.VMEM((2, 2, cap, feat), low),
-            pltpu.VMEM((slots, feat), low), pltpu.VMEM((2, 256, 2 * feat), low),
+            pltpu.VMEM((slots, feat), low), pltpu.VMEM((hidden, feat), low), pltpu.VMEM((hidden, feat), low),
+            pltpu.VMEM((far,) + shard.shape, low), pltpu.VMEM((far,) + shard.shape, low), pltpu.VMEM((far,) + shard.shape, low),
             dma((ex_size,)), dma((ex_size,)), dma((ex_size,)), dma((ex_size,)),
             dma((far,)), dma((far,)), dma((far,)), dma((far,)),
-            dma((5,)), dma((2, 2)), dma((ex_size,)), dma((3,)), dma((2,)),
+            dma((5,)), dma((2, 2)), dma((ex_size,)), dma((3,)), dma((1,)),
+            dma((far,)), dma((far,)), dma((far,)), dma((far,)),
         ],
         compiler_params=pltpu.CompilerParams(collective_id=1, has_side_effects=True, vmem_limit_bytes=60 << 20),
         name="experts",
@@ -294,7 +362,7 @@
                   gain2_ref, wqkv_hbm, wo_hbm, shard_hbm,
                   rows_hbm, fgrad_hbm, agrad_hbm, win_hbm, proj_hbm, prob_hbm, attt_hbm, normt_hbm, mixed_ref, place_ref,
                   count_ref,
-                  wqkv_v, wo_v, norm_v, normt_v, proj_v, prob_v, attt_v, att_v, bias_v, grad_v, rows_v, place_v,
+                  wqkv_v, wo_v, norm_v, normt_v, proj_v, prob_v, attt_v, att_v, bias_v, grad_v, rows_v, place_v, shard_v,
                   send_g, recv_g, send_w, recv_w, fwd_w, got_w, load_sem, store_sem, prob_sem):
     dp = lax.axis_index("dp")
     ex = lax.axis_index("expert")
@@ -312,7 +380,7 @@
     mine = win_hbm.at[pl.ds(pl.multiple_of(dp * shard, shard), shard)]
     loads = [pltpu.make_async_copy(wqkv_hbm, wqkv_v, load_sem.at[0]),
              pltpu.make_async_copy(wo_hbm, wo_v, load_sem.at[1]),
-             pltpu.make_async_copy(shard_hbm, mine, load_sem.at[2])]
+             pltpu.make_async_copy(shard_hbm, shard_v, load_sem.at[2])]
     for copy in loads:
         copy.start()
 
@@ -380,6 +448,9 @@
     for copy in stores:
         copy.start()
 
+    loads[2].wait()
+    stores.append(pltpu.make_async_copy(shard_v, mine, store_sem.at[6]))
+    stores[-1].start()
     whole = tok_ref[...].astype(jnp.float32)
     centred = whole - jnp.mean(whole, axis=1, keepdims=True)
     scale = lax.rsqrt(jnp.mean(centred * centred, axis=1, keepdims=True) + 1e-05)
@@ -475,7 +546,6 @@
         pltpu.make_async_copy(prob_v.at[pl.ds(2 * p, 2)], prob_hbm.at[pl.ds(2 * p, 2)], prob_sem.at[p]).wait()
     for copy in stores:
         copy.wait()
-    loads[2].wait()
     for copy in weight_copies:
         copy.wait_send()
     beside.wait()
@@ -509,8 +579,9 @@
             pltpu.VMEM((heads, count + count // 2, count // 2), low), pltpu.VMEM((feat, count), low),
             pltpu.VMEM((count, feat), low), pltpu.VMEM((count, count), jnp.float32),
             pltpu.VMEM((kinds, cap, feat), low), pltpu.VMEM((kinds, cap, feat), low), pltpu.VMEM((8, count), jnp.float32),
+            pltpu.VMEM(shard.shape, low),
             dma((ex_size,)), dma((ex_size,)), dma((far,)), dma((far,)), dma((far,)), dma((far,)),
-            dma((3,)), dma((6,)), dma((feat // 128,)),
+            dma((3,)), dma((7,)), dma((feat // 128,)),
         ],
         compiler_params=pltpu.CompilerParams(collective_id=0, has_side_effects=True, vmem_limit_bytes=56 << 20),
         name="attend",
@@ -523,34 +594,39 @@
         self.chunks, self.blocks, self.acc, self.got, self.out = chunks, blocks, acc, got, out
         self.sems = (ssem, rsem, gsem, hsem)
         self.offs = [[base] for base, _, _, _ in chunks]
+        self.lens = [[rows] for _, rows, _, _ in chunks]
         self.land = [[base] for base, _, _, _ in chunks]
         self.copies = [None] * len(chunks)
+        self.shift = [0] * len(chunks)
         self.stage = [0] * len(chunks)
-        self.sent = []
 
     def scatter(self, c, i):
-        base, rows, order, _ = self.chunks[c]
-        bit, peer = partner_of(order[i])
-        half = rows >> (i + 1)
-        source = self.blocks if i == 0 else self.acc
-        give = pl.multiple_of(self.offs[c][i] + (1 - bit) * half, 16)
-        copy = pltpu.make_async_remote_copy(
-            src_ref=source.at[pl.ds(give, half)], dst_ref=self.got.at[pl.ds(self.land[c][i], half)],
-            send_sem=self.sems[0].at[c, i], recv_sem=self.sems[1].at[c, i], device_id=peer, device_id_type=MESH)
-        copy.start()
-        self.offs[c].append(self.offs[c][i] + bit * half)
-        self.land[c].append(self.land[c][i] + half)
-        self.copies[c] = copy
+        base, _, order, _ = self.chunks[c]
+        mine, peers = group_of(order[i])
+        part = self.lens[c][i] >> len(order[i])
+        source = self.acc if i else self.blocks
+        self.copies[c] = []
+        for m, peer in enumerate(peers, 1):
+            give = pl.multiple_of(self.offs[c][i] + (mine ^ m) * part + self.shift[c], 16)
+            copy = pltpu.make_async_remote_copy(
+                src_ref=source.at[pl.ds(give, part)], dst_ref=self.got.at[pl.ds(self.land[c][i] + (m - 1) * part, part)],
+                send_sem=self.sems[0].at[c, i, m], recv_sem=self.sems[1].at[c, i, m], device_id=peer, device_id_type=MESH)
+            copy.start()
+            self.copies[c].append(copy)
+        self.offs[c].append(self.offs[c][i] + mine * part)
+        self.lens[c].append(part)
+        self.land[c].append(self.land[c][i] + len(peers) * part)
 
     def gather(self, c, i):
-        base, rows, order, _ = self.chunks[c]
-        _, peer = partner_of(order[i])
-        at = pl.ds(pl.multiple_of(self.offs[c][i + 1], 16), rows >> (i + 1))
-        copy = pltpu.make_async_remote_copy(
-            src_ref=self.out.at[at], dst_ref=self.out.at[at],
-            send_sem=self.sems[2].at[c, i], recv_sem=self.sems[3].at[c, i], device_id=peer, device_id_type=MESH)
-        copy.start()
-        self.copies[c] = copy
+        _, peers = group_of(self.chunks[c][2][i])
+        at = pl.ds(pl.multiple_of(self.offs[c][i + 1], 16), self.lens[c][i + 1])
+        self.copies[c] = []
+        for m, peer in enumerate(peers, 1):
+            copy = pltpu.make_async_remote_copy(
+                src_ref=self.out.at[at], dst_ref=self.out.at[at],
+                send_sem=self.sems[2].at[c, i, m], recv_sem=self.sems[3].at[c, i, m], device_id=peer, device_id_type=MESH)
+            copy.start()
+            self.copies[c].append(copy)
 
     def start(self, phase):
         for c, chunk in enumerate(self.chunks):
@@ -558,35 +634,44 @@
                 self.scatter(c, 0)
 
     def advance(self, c):
-        if self.copies[c] is None:
+        if not self.copies[c]:
             return
-        base, rows, order, _ = self.chunks[c]
-        steps, s = len(order), self.stage[c]
-        self.copies[c].wait()
+        base, _, order, _ = self.chunks[c]
+        stages, s = len(order), self.stage[c]
+        for copy in self.copies[c]:
+            copy.wait()
         self.stage[c] += 1
-        if s >= steps:
-            i = 2 * steps - 1 - s
+        if s >= stages:
+            i = 2 * stages - 1 - s
+            self.copies[c] = None
             if i > 0:
                 self.gather(c, i - 1)
-            else:
-                self.copies[c] = None
             return
-        half = rows >> (s + 1)
-        source = self.blocks if s == 0 else self.acc
-        target = self.acc if s + 1 < steps else self.out
+        part = self.lens[c][s + 1]
+        source = self.acc if s else self.blocks
+        target = self.acc if s + 1 < stages else self.out
         keep, begin = self.offs[c][s + 1], self.land[c][s]
-        tile = half
-        while tile > 128 or half % tile or tile % 16:
+        count = (1 << len(order[s])) - 1
+        tile = part
+        while tile > 128 or part % tile or tile % 16:
             tile -= 16
+        move_in = self.shift[c]
+        if s == 0:
+            self.shift[c] = base // 2 - keep
+        move_out = self.shift[c] if s + 1 < stages else 0
 
         def add(j, _):
-            at = pl.ds(pl.multiple_of(keep + j * tile, 16), tile)
-            other = self.got[pl.ds(pl.multiple_of(begin + j * tile, 16), tile), :]
-            target[at, :] = (source[at, :].astype(jnp.float32) + other.astype(jnp.float32)).astype(jnp.bfloat16)
+            at = pl.ds(pl.multiple_of(keep + move_out + j * tile, 16), tile)
+            come = pl.ds(pl.multiple_of(keep + move_in + j * tile, 16), tile)
+            total = source[come, :].astype(jnp.float32)
+            for m in range(count):
+                other = pl.ds(pl.multiple_of(begin + m * part + j * tile, 16), tile)
+                total = total + self.got[other, :].astype(jnp.float32)
+            target[at, :] = total.astype(jnp.bfloat16)
             return 0
 
-        lax.fori_loop(0, half // tile, add, 0)
-        if s + 1 < steps:
+        lax.fori_loop(0, part // tile, add, 0)
+        if s + 1 < stages:
             self.scatter(c, s + 1)
         else:
             self.gather(c, s)
@@ -596,25 +681,25 @@
             self.advance(c)
 
     def finish(self):
-        while any(copy is not None for copy in self.copies):
+        while any(self.copies):
             self.tick()
 
 
 def sum_chunks(dp_size, ex_size, rows):
     core, xs, ys, zs = butterfly(dp_size, ex_size)
-    yxz, yzx, xyz = [core] + ys + xs + zs, [core] + ys + zs + xs, [core] + xs + ys + zs
+    yxz, xyz, zyx = [[core], ys, xs, zs], [[core], xs, ys, zs], [[core], zs, ys, xs]
     if dp_size * ex_size * 16 <= 512:
-        return [(0, 1536, yxz, 0), (1536, 2048, yzx, 1), (3584, 1024, xyz, 2), (4608, 1536, yxz, 2)]
+        return [(0, 1536, yxz, 0), (1536, 2048, yxz, 1), (3584, 1024, yxz, 2), (4608, 1024, xyz, 2), (5632, 512, zyx, 2)]
     third = rows // 3
-    return [(0, third, yxz, 2), (third, third, yzx, 2), (2 * third, third, xyz, 2)]
-
-
-def unwind_kernel(dp_size, ex_size, kinds, cap, back_hbm, res_hbm, proj_hbm, prob_hbm, attt_hbm, normt_hbm, wqkv_hbm, wo_hbm,
+    return [(0, third, yxz, 2), (third, third, xyz, 2), (2 * third, third, zyx, 2)]
+
+
+def unwind_kernel(dp_size, ex_size, kinds, cap, dwo_hbm, back_hbm, res_hbm, proj_hbm, prob_hbm, attt_hbm, normt_hbm, wqkv_hbm, wo_hbm,
                   mixed_ref, tok_ref, cot_ref, place_ref, gates_ref, count_ref, gain1_ref, gain2_ref,
-                  out_ref, dtok_ref, total_ref, sum_ref,
+                  out_ref, dtok_ref, qkv_hbm, wide_hbm, sum_ref, dwout_ref,
                   back_v, ret_v, pick_v, other_v, g_v, mg_v, branch_v, da_v, dqt_v, proj_v, prob_v, attt_v, normt_v, wqkv_v,
-                  wo_v, pg_v, blocks_v, acc_v, got_v, gain_v, small_v, send_res, recv_res, ssem, rsem, gsem, hsem, tsem, usem,
-                  load_sem):
+                  wo_v, pg_v, blocks_v, acc_v, got_v, gain_v, small_v, total_ref, own_v, core_v, pre_v, chip_v, send_res, recv_res, ssem, rsem, gsem, hsem, tsem, usem,
+                  load_sem, *scatter_sems):
     dp = lax.axis_index("dp")
     ex = lax.axis_index("expert")
     count, feat = tok_ref.shape
@@ -622,19 +707,18 @@
     padded = back_v.shape[0]
     low = jnp.bfloat16
     steps = (dp_size * ex_size).bit_length() - 1
-    bits = dp_size.bit_length() - 1
 
     barrier = pltpu.get_barrier_semaphore()
     for r in range(1, ex_size):
         pl.semaphore_signal(barrier, inc=1, device_id=(dp, ex ^ r), device_id_type=MESH)
-    for k in range(bits):
-        pl.semaphore_signal(barrier, inc=1, device_id=(dp ^ (1 << k), ex), device_id_type=MESH)
+    for k in range(1, dp_size):
+        pl.semaphore_signal(barrier, inc=1, device_id=(dp ^ k, ex), device_id_type=MESH)
     loads = [pltpu.make_async_copy(source, target, load_sem.at[i]) for i, (source, target) in enumerate([
         (back_hbm, back_v.at[pl.ds(0, slots)]), (attt_hbm, attt_v), (wo_hbm, wo_v), (prob_hbm, prob_v), (proj_hbm, proj_v),
         (normt_hbm, normt_v), (wqkv_hbm, wqkv_v)])]
     for copy in loads:
         copy.start()
-    pl.semaphore_wait(barrier, ex_size - 1 + bits)
+    pl.semaphore_wait(barrier, ex_size - 1 + dp_size - 1)
     results = []
     for r in reversed(range(1, ex_size)):
         copy = pltpu.make_async_remote_copy(
@@ -648,6 +732,18 @@
     results.append(pltpu.make_async_copy(res_hbm.at[pl.ds(0, 2 * cap)], ret_v.at[pl.ds(0, 2 * cap)], load_sem.at[8]))
     for copy in results[-2:]:
         copy.start()
+    far = dp_size // 2
+    shard = dwout_ref.shape[0]
+    scatter = Scatter(dp, ex, far, core_v, pre_v, chip_v, scatter_sems)
+
+    def shard_at(which):
+        return dwo_hbm.at[pl.ds(pl.multiple_of(which * shard, shard), shard)]
+
+    for k in list(range(1, far)) + [0]:
+        scatter.to_core(k, shard_at(dp ^ (2 * k + 1)))
+    own_copies = [pltpu.make_async_copy(shard_at(dp ^ (2 * k)), own_v.at[k], load_sem.at[9 + k]) for k in range(far)]
+    for copy in own_copies:
+        copy.start()
     if padded > slots:
         ret_v[slots:, :] = jnp.zeros((padded - slots, feat), low)
         back_v[slots:, :] = jnp.zeros((padded - slots, feat), low)
@@ -672,6 +768,10 @@
         return 0
 
     lax.fori_loop(0, feat // 256, collect, 0)
+    for copy in own_copies:
+        copy.wait()
+    for k in range(1, far):
+        scatter.to_chip(k, own_v.at[k])
     gain_v[...] = jnp.zeros_like(gain_v)
     gain_v[16:24, 0:128] = count_ref[...]
 
@@ -787,21 +887,31 @@
     order = sums.chunks[0][2]
 
     def small_send(i):
-        _, peer = partner_of(order[i])
-        copy = pltpu.make_async_remote_copy(
-            src_ref=small_v.at[steps + i], dst_ref=small_v.at[i], send_sem=tsem.at[i], recv_sem=usem.at[i],
-            device_id=peer, device_id_type=MESH)
-        copy.start()
-        return copy
-
-    def small_add(i, copy):
-        copy.wait()
-        total = small_v[steps + i] + small_v[i]
-        if i + 1 < steps:
+        copies = []
+        for m, peer in enumerate(group_of(order[i])[1], 1):
+            copy = pltpu.make_async_remote_copy(
+                src_ref=small_v.at[steps + i], dst_ref=small_v.at[slot_of[i] + m - 1], send_sem=tsem.at[i, m],
+                recv_sem=usem.at[i, m], device_id=peer, device_id_type=MESH)
+            copy.start()
+            copies.append(copy)
+        return copies
+
+    def small_add(i, copies):
+        for copy in copies:
+            copy.wait()
+        mine, peers = group_of(order[i])
+        total = jnp.zeros_like(sum_ref[...])
+        for n in range(len(peers) + 1):
+            term = small_v[steps + i]
+            for m in range(1, len(peers) + 1):
+                term = jnp.where(mine == n ^ m, small_v[slot_of[i] + m - 1], term)
+            total = total + term
+        if i + 1 < len(order):
             small_v[steps + i + 1] = total
             return small_send(i + 1)
         sum_ref[...] = total
 
+    slot_of = [steps + len(order) + sum((1 << len(stage)) - 1 for stage in order[:i]) for i in range(len(order))]
     tiny = small_send(0)
     sums.tick()
     for copy in results:
@@ -823,13 +933,22 @@
         return 0
 
     lax.fori_loop(0, feat // 256, deliver, 0)
-    for i in range(steps):
+    scatter.total(own_v.at[0], dwout_ref)
+    for i in range(len(order)):
         sums.tick()
         tiny = small_add(i, tiny)
     sums.finish()
-
-
-def unwind(back, res, proj, prob, attt, normt, wqkv, wo, mixed, tokens, cotangent, place, gates, tally, gain1, gain2,
+    finals = []
+    for b in range(8):
+        turn, c = (b - 2) // 3, (b - 2) % 3
+        target = wide_hbm.at[:, pl.ds(b * wide, wide)] if b < 2 else qkv_hbm.at[:, pl.ds(c * feat + turn * wide, wide)]
+        finals.append(pltpu.make_async_copy(total_ref.at[pl.ds(b * feat, feat)], target, load_sem.at[b]))
+        finals[-1].start()
+    for copy in finals:
+        copy.wait()
+
+
+def unwind(dwo, back, res, proj, prob, attt, normt, wqkv, wo, mixed, tokens, cotangent, place, gates, tally, gain1, gain2,
            dp_size, ex_size):
     kinds, cap, feat = back.shape
     count = tokens.shape[0]
@@ -844,11 +963,14 @@
     low, full = jnp.bfloat16, jnp.float32
     shape = jax.ShapeDtypeStruct
     chunks = len(sum_chunks(dp_size, ex_size, rows))
+    stages = 4
+    shard, far = dwo.shape[0] // dp_size, dp_size // 2
     return pl.pallas_call(
         functools.partial(unwind_kernel, dp_size, ex_size, kinds, cap),
-        out_shape=(shape((count, feat), low), shape((count, feat), low), shape((rows, wide), low), shape((8, feat), full)),
-        in_specs=[anyspace] * 8 + [vmem] * 8,
-        out_specs=(vmem,) * 4,
+        out_shape=(shape((count, feat), low), shape((count, feat), low), shape((feat, 3 * feat), low), shape((feat, feat), low), shape((8, feat), full),
+                   shape((shard, feat), full)),
+        in_specs=[anyspace] * 9 + [vmem] * 8,
+        out_specs=(vmem, vmem, anyspace, anyspace, vmem, vmem),
         scratch_shapes=[
             pltpu.VMEM((padded, feat), low), pltpu.VMEM((padded, feat), low), pltpu.VMEM((count, padded), low),
             pltpu.VMEM((count, padded), low), pltpu.VMEM((count, feat), full), pltpu.VMEM((count, feat), full),
@@ -856,14 +978,16 @@
             pltpu.VMEM((count, 3 * feat), low), pltpu.VMEM((heads, count + count // 2, count // 2), low),
             pltpu.VMEM((feat, count), low), pltpu.VMEM((feat, count), low), pltpu.VMEM((feat, 3 * feat), low),
             pltpu.VMEM((feat, feat), low), pltpu.VMEM((count, 3 * feat), low), pltpu.VMEM((rows, wide), low),
-            pltpu.VMEM((rows, wide), low), pltpu.VMEM((rows, wide), low), pltpu.VMEM((24, feat), full),
-            pltpu.VMEM((2 * steps, 8, feat), full),
-            dma((ex_size,)), dma((ex_size,)), dma((chunks, steps)), dma((chunks, steps)), dma((chunks, steps)),
-            dma((chunks, steps)), dma((steps,)), dma((steps,)), dma((9,)),
+            pltpu.VMEM((rows // 2, wide), low), pltpu.VMEM((rows, wide), low), pltpu.VMEM((24, feat), full),
+            pltpu.VMEM((steps + stages + 3 * stages, 8, feat), full), pltpu.VMEM((rows, wide), low), pltpu.VMEM((far, shard, feat), low), pltpu.VMEM((far, shard, feat), low),
+            pltpu.VMEM((far, shard, feat), low), pltpu.VMEM((far, shard, feat), low),
+            dma((ex_size,)), dma((ex_size,)), dma((chunks, stages, 4)), dma((chunks, stages, 4)),
+            dma((chunks, stages, 4)), dma((chunks, stages, 4)), dma((stages, 4)), dma((stages, 4)), dma((9 + far,)),
+            dma((far,)), dma((far,)), dma((far,)), dma((far,)),
         ],
         compiler_params=pltpu.CompilerParams(collective_id=2, has_side_effects=True, vmem_limit_bytes=62 << 20),
         name="unwind",
-    )(back.reshape(slots, feat), res.reshape(slots, feat), proj, prob, attt, normt, wqkv, wo, mixed, tokens, cotangent,
+    )(dwo, back.reshape(slots, feat), res.reshape(slots, feat), proj, prob, attt, normt, wqkv, wo, mixed, tokens, cotangent,
       place, gates, tally, gain1, gain2)
 
 
@@ -894,26 +1018,20 @@
     rows, fgrad, agrad, weights_in, projected, probs_t, attended_t, norm_t, mixed_rows, place, tally = attend(
         tokens, cotangent, chosen, gates, lengths, keep_mask, gain1, gain2, w_qkv, w_o, w_in[0], kind_count, slot_count,
         dp_size, owners)
-    row_grads, served, weight_grads = experts(
+    row_grads, served, out_grads, d_w_in = experts(
         rows, fgrad, agrad, weights_in, w_out[0], frozen_in, frozen_out, dp_size, owners)
-    summed = lax.psum_scatter(weight_grads, "dp", scatter_dimension=0, tiled=True).astype(jnp.float32)
-    d_w_in = summed[:, :feat_width][None]
-    d_w_out = summed[:, feat_width:][None]
-    output, tokens_grad, total, small_sum = unwind(
-        row_grads, served, projected, probs_t, attended_t, norm_t, w_qkv, w_o, mixed_rows, tokens, cotangent, place, gates,
-        tally, gain1, gain2, dp_size, owners)
-    blocks = total.reshape(8, feat_width, feat_width // 2).astype(jnp.float32)
-    w_o_sum = jnp.concatenate([blocks[0], blocks[1]], axis=1)
-    w_qkv_sum = jnp.concatenate([blocks[i] for i in (2, 5, 3, 6, 4, 7)], axis=1)
+    output, tokens_grad, w_qkv_sum, w_o_sum, small_sum, d_w_out = unwind(
+        out_grads, row_grads, served, projected, probs_t, attended_t, norm_t, w_qkv, w_o, mixed_rows, tokens, cotangent, place,
+        gates, tally, gain1, gain2, dp_size, owners)
     return (
         output,
         tokens_grad,
         small_sum[0],
-        w_qkv_sum,
-        w_o_sum,
+        w_qkv_sum.astype(jnp.float32),
+        w_o_sum.astype(jnp.float32),
         small_sum[1],
-        d_w_in,
-        d_w_out,
+        d_w_in[None],
+        d_w_out[None],
         small_sum[2, :kind_count],
     )
 

time: 283 us -> 259 us (0.915)
  between operations: 14.1 us -> 0.68 us
  Pallas kernels: 246 us -> 241 us
  local copies, waits for them, and re-layouts: 15.2 us -> 10.4 us
    pallas_call x1, Pallas kernels: 114 us -> 95.4 us  [unwind(): pl.pallas_call(functools.partial(unwind_kernel, dp_size, ex_size, kinds,...]
    pallas_call x1, Pallas kernels: 84.8 us -> 98.9 us  [experts(): pl.pallas_call(functools.partial(expert_kernel, dp_size, ex_size, cap), o...]
    unnamed x16 -> x15, local copies, waits for them, and re-layouts: 8.73 us -> 7.66 us
  transfers between devices with their start and end apart: 1 -> 0, of which waited for: 0 -> 0; matrix products, arithmetic and copies ran while one was open for 5% -> 0% of each run, Pallas kernels for 41% -> 0%
where the time goes in v2:
time: 259 us; the launch traced here: 258 us
  Pallas kernels  241 us (93%)
  local copies, waits for them, and re-layouts  10.4 us (4%)
  other arithmetic  6.32 us (2%)
    pallas_call x1, Pallas kernels, experts(): pl.pallas_call(functools.partial(expert_kernel, dp_size, ex_size, cap), o...  98.9 us
    pallas_call x1, Pallas kernels, unwind(): pl.pallas_call(functools.partial(unwind_kernel, dp_size, ex_size, kinds,...  95.4 us
    pallas_call x1, Pallas kernels, attend(): pl.pallas_call(functools.partial(attend_kernel, dp_size, ex_size, kinds,...  46.6 us
    unnamed x15, local copies, waits for them, and re-layouts  7.66 us

profile of v2, /device:TPU:0, one launch (start us, length us, event | category | flops | bytes accessed | tf_op | source)
XLA Modules:
  0.0 258.3 jit_solution(14838598678831146769)
XLA Ops:
  0.6 1.5 copy.23.gates_ref
  2.2 46.6 %attend.1 = (bf16[10,128,768]{2,1,0:T(8,128)(2,1)}, bf16[2,128,768]{2,1,0:T(8,128)(2,1)}, bf16[8,128,768]{2,1,0:T(8,128)(2,1)}, bf16[3072,768]{1,0:T(8,128)(2,1)...) custom-call(s32[1,8]{1,0:T(1,128)} %lengths_s.1, ...), custom_call_target="tpu_custom_call" | custom-call | tf_op jit(solution)/shard_map/attend/pallas_call | solution.py:567
  48.8 98.9 %experts.1 = (bf16[10,128,768]{2,1,0:T(8,128)(2,1)}, bf16[10,128,768]{2,1,0:T(8,128)(2,1)}, bf16[3072,768]{1,0:T(8,128)(2,1)}, f32[768,768]{1,0:T(8,128)}) custom-call(bf16[10,128,768]{2,1,0:T(8,128)(2,1)} %get-tuple-element.30.rows_hbm, bf16[2,128,768]{2,1,0:T(8,128)(2,1)} %get-tuple-element.31.fgrad_hbm, bf16[8,128,768]{2,1,0:T(8,128)(2,1)} %get-tuple-element.32.agrad_hbm, ...), custom_call_target="tpu_custom_call" | custom-call | tf_op jit(solution)/shard_map/experts/pallas_call | solution.py:336
  147.7 95.4 %unwind.1 = (bf16[512,768]{1,0:T(8,128)(2,1)}, bf16[512,768]{1,0:T(8,128)(2,1)}, bf16[768,2304]{1,0:T(8,128)(2,1)}, bf16[768,768]{1,0:T(8,128)(2,1)}, f32[8,768]{1,0:T(8,128)}, /*index=5*/f32[768,768]{1,0:T(8,128)}) custom-call(bf16[3072,768]{1,0:T(8,128)(2,1)} %get-tuple-element.34.dwo_hbm, bf16[1280,768]{1,0:T(8,128)(2,1)} %bitcast.17, ...), custom_call_target="tpu_custom_call" | custom-call | tf_op jit(solution)/shard_map/unwind/pallas_call | solution.py:968
  243.1 0.0 copy-start
  243.1 1.3 slice_bitcast_fusion
  244.4 1.4 slice_reduce_fusion
  245.9 2.8 %convert_element_type.7 = f32[768,768]{1,0:T(8,128)} convert(bf16[768,768]{1,0:T(8,128)(2,1)} %get-tuple-element.48) | non-fusion elementwise | flops 589824 | bytes 3538944 | tf_op jit(solution)/shard_map/convert_element_type | solution.py:1031
  248.7 0.0 copy-done
  248.7 0.0 copy-start.4
  248.7 0.0 copy-start.3
  248.7 3.5 %convert_element_type.6 = f32[768,2304]{1,0:T(8,128)} convert(bf16[768,2304]{1,0:T(8,128)(2,1)S(1)} %copy-done) | non-fusion elementwise | flops 1769472 | bytes 10616832 | tf_op jit(solution)/shard_map/convert_element_type | solution.py:1030
  252.2 0.0 copy-done.4
  252.2 0.0 copy-start.1
  252.2 0.9 copy.28
  253.1 0.0 copy-done.3
  253.1 0.9 copy.29
  254.0 0.4 copy-done.1
  254.4 0.0 copy-start.2
  254.4 1.4 copy.30
  255.8 1.1 copy-done.2
  256.9 1.4 copy.31
Async XLA Ops:
  243.1 5.6 %copy-start = (bf16[768,2304]{1,0:T(8,128)(2,1)S(1)}, bf16[768,2304]{1,0:T(8,128)(2,1)}, u32[]{:S(2)}) copy-start(bf16[768,2304]{1,0:T(8,128)(2,1)} %get-tuple-element.47) | copy-start | bytes 10616836
  248.7 3.5 %copy-start.4 = (bf16[512,768]{1,0:T(8,128)(2,1)S(1)}, bf16[512,768]{1,0:T(8,128)(2,1)}, u32[]{:S(2)}) copy-start(bf16[512,768]{1,0:T(8,128)(2,1)} %get-tuple-element.62) | copy-start | bytes 2359300
  248.7 4.4 %copy-start.3 = (bf16[512,768]{1,0:T(8,128)(2,1)S(1)}, bf16[512,768]{1,0:T(8,128)(2,1)}, u32[]{:S(2)}) copy-start(bf16[512,768]{1,0:T(8,128)(2,1)} %get-tuple-element.63) | copy-start | bytes 2359300
  252.2 2.2 copy-start.1
  254.4 2.5 copy-start.2
